TPU v7x, 32 devices: a whole 2x2x4 slice. The times are simulated.
32 devices in a mesh: grp: 2 (over x), row: 16 (over z, y, core).
Axes of the slice: x: 2, y: 2, z: 4, core: 2. Of those that a mesh axis runs over, the one named last changes fastest.
Arguments:
- start: float32 [3, 262144], P(None, ('grp', 'row')), parts along dimension 1, may hold values from -6 to 6
- rhs: float32 [3, 262144], P(None, ('grp', 'row')), parts along dimension 1, may hold values from -6 to 6
- fine_vals: bfloat16 [3, 3, 12, 262144], P(None, None, None, ('grp', 'row')), parts along dimension 3
- fine_cols: int32 [12, 262144], P(None, ('grp', 'row')), parts along dimension 1, may hold values from 0 to 16383, as said below
- prol: bfloat16 [3, 3, 262144], P(None, None, ('grp', 'row')), parts along dimension 2, may hold values from -3 to 3
- aggregate: int32 [262144], P(('grp', 'row')), parts along dimension 0, may hold values from 0 to 8191, as said below
- coarse_vals: bfloat16 [3, 3, 12, 16384], P(None, None, None, ('grp', 'row')), parts along dimension 3
- coarse_cols: int32 [12, 16384], P(None, ('grp', 'row')), parts along dimension 1, may hold values from 0 to 1023, as said below
Outputs:
- fine_iterate: float32 [3, 262144], P(None, ('grp', 'row')), parts along dimension 1
- coarse_iterate: float32 [3, 16384], P(None, ('grp', 'row')), parts along dimension 1
- coarse_residual: float32 [3, 16384], P(None, ('grp', 'row')), parts along dimension 1
There are 2 independent parts, one for each index of `grp`. A program takes and returns all parts, laid end to end along the dimension named above; each array names one. Nothing has to cross between parts.
Inputs may be any that keep to these rules, and one draw needn't show every extreme that they name: `fine_cols`: slot 0 of every row holds 4096 + the node's position on its device; every index is a position in a device's 8192 nodes extended by 4096 nodes of each neighbouring device on either side (position 0 is the first of the lower neighbour's last 4096 nodes). `coarse_cols`: slot 0 of every row holds 256 + the aggregate's position on its device; every index is a position in a device's 512 aggregates extended by 256 aggregates of each neighbouring device on either side. A fine node of device block d lies in an aggregate from 512 * d - 16 to 512 * (d + 1) + 15.
All inputs are finite; a program needn't handle non-finite values.
Results may differ from a plain program's by a relative error of at most 0.0003.
Values sent between devices are 32-bit elements; how exact they have to be, the bound alone decides.
A program may use at most 128 MiB of HBM per device.

v0:
```python
import jax
import jax.numpy as jnp
from jax import lax
from jax.sharding import PartitionSpec as P

LAYER = 4096
NC = 512


lower_fraction = 0.1


def padded(block, sides, width):
    for axis, dim in sides:
        count = lax.axis_size(axis)
        forward = [(i, i + 1) for i in range(count - 1)]
        backward = [(target, source) for source, target in forward]
        low = lax.ppermute(
            lax.slice_in_dim(block, block.shape[dim] - width, None, axis=dim), axis, forward
        )
        high = lax.ppermute(lax.slice_in_dim(block, 0, width, axis=dim), axis, backward)
        block = jnp.concatenate([low, block, high], axis=dim)
    return block


def from_behind(value, axis, by):
    size = lax.axis_size(axis)
    pairs = [(i, i + by) for i in range(size) if 0 <= i + by < size]
    return lax.ppermute(value, axis, pairs)


def local_apply(extended, values, columns):
    gathered = extended[:, columns]
    return jnp.sum(values.astype(jnp.float32) * gathered[None], axis=(1, 2))


def diag_inverse(values):
    return 1.0 / jnp.stack([values[c, c, 0] for c in range(3)]).astype(jnp.float32)


def local_bound(values, inverse):
    return jnp.max(jnp.sum(jnp.abs(values.astype(jnp.float32)), axis=(1, 2)) * inverse)


def coefficients(bound):
    lowest = lower_fraction * bound
    theta = (bound + lowest) / 2.0
    delta = (bound - lowest) / 2.0
    sigma = theta / delta
    rho_zero = 1.0 / sigma
    rho_one = 1.0 / (2.0 * sigma - rho_zero)
    return (theta, delta, rho_zero, rho_one)


def chebyshev(operator, inverse, iterate, residual, bound):
    theta, delta, rho_zero, rho_one = coefficients(bound)
    first = inverse * residual / theta
    iterate = iterate + first
    residual = residual - operator(first)
    second = rho_one * rho_zero * first + 2.0 * rho_one / delta * inverse * residual
    iterate = iterate + second
    residual = residual - operator(second)
    return (iterate, residual)


def shards(start, rhs, fine_vals, fine_cols, prol, aggregate, coarse_vals, coarse_cols):

    def fine_apply(vector):
        extended = padded(vector, (("row", 1),), LAYER)
        return local_apply(extended, fine_vals, fine_cols)

    def coarse_apply(vector):
        extended = padded(vector, (("row", 1),), NC // 2)
        return local_apply(extended, coarse_vals, coarse_cols)

    dinv = diag_inverse(fine_vals)
    cdinv = diag_inverse(coarse_vals)
    fine_local = local_bound(fine_vals, dinv)
    bound = lax.pmax(fine_local, "row")
    residual = rhs - fine_apply(start)
    fine_iterate, fine_res = chebyshev(fine_apply, dinv, start, residual, bound)
    contrib = jnp.sum(prol.astype(jnp.float32) * fine_res[:, None, :], axis=0)
    offset = lax.axis_index("row") * NC
    position = aggregate - offset + NC
    partial_sums = jnp.zeros((3, 3 * NC), jnp.float32).at[:, position].add(contrib)
    from_above = from_behind(partial_sums[:, :NC], "row", -1)
    from_below = from_behind(partial_sums[:, 2 * NC :], "row", 1)
    restricted = partial_sums[:, NC : 2 * NC] + from_above + from_below
    cbound = lax.pmax(local_bound(coarse_vals, cdinv), "row")
    zeros = jnp.zeros_like(restricted)
    coarse_iterate, coarse_residual = chebyshev(coarse_apply, cdinv, zeros, restricted, cbound)
    return (fine_iterate, coarse_iterate, coarse_residual)


def solution(mesh):
    in_specs = (
        P(None, ("grp", "row")),
        P(None, ("grp", "row")),
        P(None, None, None, ("grp", "row")),
        P(None, ("grp", "row")),
        P(None, None, ("grp", "row")),
        P(("grp", "row")),
        P(None, None, None, ("grp", "row")),
        P(None, ("grp", "row")),
    )
    out_specs = (P(None, ("grp", "row")), P(None, ("grp", "row")), P(None, ("grp", "row")))
    return jax.shard_map(shards, mesh=mesh, in_specs=in_specs, out_specs=out_specs, check_vma=False)
```

profile of v0, /device:TPU:7, one launch (start us, length us, event | category | flops | bytes accessed | tf_op | source)
XLA Modules:
  0.0 1269.9 jit_solution(3382095957612516674)
XLA Ops:
  1.5 2.6 collective-permute-start.1
  4.1 3.9 collective-permute-start
  13.7 5.0 copy.101
  18.7 326.4 %gather_fusion = f32[98304,3]{1,0:T(8,128)} fusion(f32[3,16384]{0,1:T(8,128)} %copy.101, s32[98304]{0:T(1024)S(1)} %broadcast_clamp_fusion), kind=kCustom, calls=%fused_computation | custom fusion | bytes 2752512 | tf_op jit(solution)/shard_map/gather | solution.py:33
  345.1 31.3 %copy.102 = f32[3,12,8192]{2,1,0:T(8,128)} copy(f32[3,12,8192]{0,2,1:T(8,128)} %bitcast.29) | data formatting | bytes 2359296 | tf_op jit(solution)/shard_map/gather | solution.py:33
  376.4 2.7 fusion.1
  379.9 23.8 %all-reduce = (f32[]{:T(128)}, f32[]{:T(128)}) all-reduce(f32[]{:T(128)} %multiply_reduce_fusion.1, f32[]{:T(128)} %multiply_reduce_fusion.2), channel_id=1, replica_groups=mesh['grp'=2,'row'=16] {'row'}, use_global_device_ids=true, to_apply=%region_3.0 | all-reduce | flops 2 | bytes 16 | tf_op jit(solution)/shard_map/pmax | solution.py:79
  405.1 5.9 collective-permute-start.3
  411.0 1.9 collective-permute-start.2
  414.9 5.0 copy.103
  419.9 326.4 %gather_fusion.1 = f32[98304,3]{1,0:T(8,128)} fusion(f32[3,16384]{0,1:T(8,128)} %copy.103, s32[98304]{0:T(1024)S(1)} %broadcast_clamp_fusion), kind=kCustom, calls=%fused_computation.1 | custom fusion | bytes 2752512 | tf_op jit(solution)/shard_map/gather | solution.py:33
  746.3 31.2 %copy.104 = f32[3,12,8192]{2,1,0:T(8,128)} copy(f32[3,12,8192]{0,2,1:T(8,128)} %bitcast.30) | data formatting | bytes 2359296 | tf_op jit(solution)/shard_map/gather | solution.py:33
  777.4 2.1 fusion.2
  780.5 7.1 collective-permute-start.5
  787.5 1.9 collective-permute-start.4
  790.8 5.0 copy.105
  795.8 326.4 %gather_fusion.2 = f32[98304,3]{1,0:T(8,128)} fusion(f32[3,16384]{0,1:T(8,128)} %copy.105, s32[98304]{0:T(1024)S(1)} %broadcast_clamp_fusion), kind=kCustom, calls=%fused_computation.2 | custom fusion | bytes 2752512 | tf_op jit(solution)/shard_map/gather | solution.py:33
  1122.3 31.2 %copy.106 = f32[3,12,8192]{2,1,0:T(8,128)} copy(f32[3,12,8192]{0,2,1:T(8,128)} %bitcast.28) | data formatting | bytes 2359296 | tf_op jit(solution)/shard_map/gather | solution.py:33
  1153.4 2.1 fusion.3
  1155.8 2.6 copy.107
  1158.4 44.5 %scatter_custom_fusion = f32[3,1536]{0,1:T(8,128)S(1)} fusion(s32[8192]{0:T(1024)S(1)} %compare_select_fusion.2, f32[8192,3]{1,0:T(8,128)} %copy.107, f32[]{:T(128)} %constant.15.clone.1), kind=kCustom, calls=%fused_computation.19 | custom fusion | flops 24576 | bytes 18944 | tf_op jit(solution)/shard_map/scatter-add | solution.py:85
  1203.1 5.2 collective-permute-start.7
  1208.4 1.9 collective-permute-start.6
  1211.8 2.5 collective-permute-done.6
  1214.3 1.9 collective-permute-start.9
  1216.2 4.5 collective-permute-start.8
  1222.7 17.1 %gather_fusion.3 = f32[6144,3]{1,0:T(8,128)S(1)} fusion(f32[3,1024]{0,1:T(8,128)} %copy.111, s32[6144]{0:T(1024)S(1)} %broadcast_clamp_fusion.1), kind=kCustom, calls=%fused_computation.3 | custom fusion | bytes 172032 | tf_op jit(solution)/shard_map/gather | solution.py:33
  1239.8 1.5 copy.112
  1242.0 1.9 collective-permute-start.11
  1243.9 5.0 collective-permute-start.10
  1250.6 17.1 %gather_fusion.4 = f32[6144,3]{1,0:T(8,128)S(1)} fusion(f32[3,1024]{0,1:T(8,128)} %copy.113, s32[6144]{0:T(1024)S(1)} %broadcast_clamp_fusion.1), kind=kCustom, calls=%fused_computation.4 | custom fusion | bytes 172032 | tf_op jit(solution)/shard_map/gather | solution.py:33
  1267.7 1.5 copy.114
  (62 shorter events, 15.5 us)
Async XLA Ops:
  1.5 11.2 collective-permute-start.1
  4.1 8.6 collective-permute-start
  345.1 31.3 %copy-start = (bf16[3,3,12,8192]{3,2,1,0:T(8,128)(2,1)S(1)}, bf16[3,3,12,8192]{3,2,1,0:T(8,128)(2,1)}, u32[]{:S(2)}) copy-start(bf16[3,3,12,8192]{3,2,1,0:T(8,128)(2,1)} %param.10) | copy-start | bytes 5308420
  345.1 59.9 %copy-start.4 = (f32[3,8192]{1,0:T(4,128)S(1)}, f32[3,8192]{1,0:T(4,128)}, u32[]{:S(2)}) copy-start(f32[3,8192]{1,0:T(4,128)} %param.9) | copy-start | bytes 294916
  405.1 8.6 collective-permute-start.3
  411.0 3.8 collective-permute-start.2
  746.3 33.3 %copy-start.2 = (f32[3,8192]{1,0:T(4,128)S(1)}, f32[3,8192]{1,0:T(4,128)}, u32[]{:S(2)}) copy-start(f32[3,8192]{1,0:T(4,128)} %param.8) | copy-start | bytes 294916
  777.4 12.0 copy-start.5
  780.5 9.0 collective-permute-start.5
  787.5 3.2 collective-permute-start.4
  1122.3 33.4 %copy-start.3 = (bf16[3,3,8192]{2,1,0:T(4,128)(2,1)S(1)}, bf16[3,3,8192]{2,1,0:T(4,128)(2,1)}, u32[]{:S(2)}) copy-start(bf16[3,3,8192]{2,1,0:T(4,128)(2,1)} %param.12) | copy-start | bytes 442372
  1155.6 54.7 %copy-start.6 = (s32[12,512]{1,0:T(8,128)S(1)}, s32[12,512]{1,0:T(8,128)}, u32[]{:S(2)}) copy-start(s32[12,512]{1,0:T(8,128)} %param.15) | copy-start | bytes 73732
  1158.4 82.9 %copy-start.1 = (bf16[3,3,12,512]{3,2,1,0:T(8,128)(2,1)S(1)}, bf16[3,3,12,512]{3,2,1,0:T(8,128)(2,1)}, u32[]{:S(2)}) copy-start(bf16[3,3,12,512]{3,2,1,0:T(8,128)(2,1)} %param.14) | copy-start | bytes 331780
  1203.1 8.7 collective-permute-start.7
  1208.4 5.9 collective-permute-start.6
  1214.3 7.3 collective-permute-start.9
  1216.2 5.4 collective-permute-start.8
  1242.0 6.9 collective-permute-start.11
  1243.9 5.7 collective-permute-start.10
where the time goes:
time: 1270 us
  local copies, waits for them, and re-layouts  1130 us (89%)
  other arithmetic  58.7 us (5%)
  starting transfers between devices  43.6 us (3%)
  blocking collectives  23.8 us (2%)
    gather x10, local copies, waits for them, and re-layouts, local_apply(): gathered = extended[:, columns]  1110 us
    scatter-add x1, other arithmetic, shards(): jnp.zeros((3, 3 * NC), jnp.float32).at[:, position].add(contrib)  44.5 us
  transfers between devices with their start and end apart: 12, of which 4 were waited for; matrix products, arithmetic and copies ran while one was open for 0% of the time, Pallas kernels for 0%

commit v1 on v0

v1 whole, which is shorter than its diff:
```python
import functools

import jax
import jax.numpy as jnp
from jax import lax
from jax.experimental import pallas as pl
from jax.experimental.pallas import tpu as pltpu
from jax.sharding import PartitionSpec as P

LANE = 128
CHUNK = 16
GROUP = 4
lower_fraction = 0.1

f32, i32, bf16 = jnp.float32, jnp.int32, jnp.bfloat16
VMEM = pl.BlockSpec(memory_space=pltpu.VMEM)
SMEM = pl.BlockSpec(memory_space=pltpu.SMEM)


def coefficients(bound):
    lowest = lower_fraction * bound
    theta = (bound + lowest) / 2.0
    delta = (bound - lowest) / 2.0
    sigma = theta / delta
    rho_zero = 1.0 / sigma
    rho_one = 1.0 / (2.0 * sigma - rho_zero)
    return (theta, delta, rho_zero, rho_one)


def at_block(b):
    if isinstance(b, int):
        return pl.ds(b * LANE, LANE)
    return pl.ds(pl.multiple_of(b * LANE, LANE), LANE)


def take_lanes(row, lanes):
    return jnp.take_along_axis(row, lanes, axis=1, mode="promise_in_bounds")


def pad_rows(x):
    return x[0:8], jnp.concatenate([x[8:12], x[8:12]], axis=0)


def halves(cols):
    parts = pad_rows(cols)
    return [p & (LANE - 1) for p in parts], [p >> 7 for p in parts]


def visit(table_ref, r, lanes, rows, acc):
    at = at_block(r)
    masks = [row == r for row in rows]
    out = []
    for j in range(3):
        src = jnp.broadcast_to(table_ref[j : j + 1, at], (8, LANE))
        for h in range(2):
            out.append(jnp.where(masks[h], take_lanes(src, lanes[h]), acc[2 * j + h]))
    return out


def contract(vals_ref, at, acc):
    out = []
    gathered = [jnp.concatenate([acc[2 * j], acc[2 * j + 1][0:4]], axis=0) for j in range(3)]
    for c in range(3):
        total = None
        for j in range(3):
            term = vals_ref[c, j, :, at].astype(f32) * gathered[j]
            total = term if total is None else total + term
        out.append(jnp.sum(total, axis=0, keepdims=True))
    return out


def bound_of_block(vals_ref, at, dinv_ref, best):
    for c in range(3):
        total = None
        for j in range(3):
            term = jnp.abs(vals_ref[c, j, :, at].astype(f32))
            total = term if total is None else total + term
        inverse = 1.0 / vals_ref[c, c, :, at].astype(f32)[0:1]
        dinv_ref[c : c + 1, at] = inverse
        best = jnp.maximum(best, jnp.sum(total, axis=0, keepdims=True) * inverse)
    return best


def neighbours(me, n):
    return ((me > 0, me - 1), (me < n - 1, me + 1))


def exchange(source, target, width, own, me, n, sends, recvs):
    low = pltpu.make_async_remote_copy(
        src_ref=source.at[:, pl.ds(0, width)],
        dst_ref=target.at[:, pl.ds(width + own, width)],
        send_sem=sends.at[0],
        recv_sem=recvs.at[0],
        device_id={"row": jnp.maximum(me - 1, 0)},
        device_id_type=pl.DeviceIdType.MESH,
    )
    high = pltpu.make_async_remote_copy(
        src_ref=source.at[:, pl.ds(own - width, width)],
        dst_ref=target.at[:, pl.ds(0, width)],
        send_sem=sends.at[1],
        recv_sem=recvs.at[1],
        device_id={"row": jnp.minimum(me + 1, n - 1)},
        device_id_type=pl.DeviceIdType.MESH,
    )

    def start():
        @pl.when(me > 0)
        def _():
            low.start()

        @pl.when(me < n - 1)
        def _():
            high.start()

        zeros = jnp.zeros((3, width), f32)

        @pl.when(me == 0)
        def _():
            target[:, pl.ds(0, width)] = zeros

        @pl.when(me == n - 1)
        def _():
            target[:, pl.ds(width + own, width)] = zeros

    def wait():
        @pl.when(me > 0)
        def _():
            low.wait_send()
            high.wait_recv()

        @pl.when(me < n - 1)
        def _():
            high.wait_send()
            low.wait_recv()

    return start, wait


def greet(me, n, everyone):
    barrier = pltpu.get_barrier_semaphore()
    if everyone:
        def one(step, carry):
            pl.semaphore_signal(
                barrier, inc=1, device_id={"row": lax.rem(me + step, n)},
                device_id_type=pl.DeviceIdType.MESH,
            )
            return carry

        lax.fori_loop(1, n, one, 0)
        pl.semaphore_wait(barrier, n - 1)
    else:
        for cond, who in neighbours(me, n):
            @pl.when(cond)
            def _():
                pl.semaphore_signal(
                    barrier, inc=1, device_id={"row": who}, device_id_type=pl.DeviceIdType.MESH
                )
        pl.semaphore_wait(barrier, jnp.minimum(me, 1) + jnp.minimum(n - 1 - me, 1))


def first_kernel(n, start_ref, vals_ref, cols_ref, cvals_ref,
                 ext_ref, lists_ref, dinv_ref, cdinv_ref, bounds_ref,
                 words, mine, theirs, sends, recvs, bsends, brecvs, own_sem):
    me = lax.axis_index("row")
    own = start_ref.shape[1]
    width = (ext_ref.shape[1] - own) // 2
    blocks, cblocks = own // LANE, cvals_ref.shape[3] // LANE
    greet(me, n, True)
    start, wait = exchange(start_ref, ext_ref, width, own, me, n, sends, recvs)
    start()
    keep = pltpu.make_async_copy(start_ref, ext_ref.at[:, pl.ds(width, own)], own_sem)
    keep.start()

    low = jnp.full((1, LANE), -jnp.inf, f32)

    def bound_step(g, best):
        for u in range(2):
            best = bound_of_block(vals_ref, at_block(g * 2 + u), dinv_ref, best)
        return best

    best = lax.fori_loop(0, blocks // 2, bound_step, low)
    cbest = low
    for b in range(cblocks):
        cbest = bound_of_block(cvals_ref, at_block(b), cdinv_ref, cbest)
    both = jnp.concatenate([jnp.broadcast_to(x, (4, LANE)) for x in (best, cbest)], axis=0)
    for shift in (64, 32, 16, 8, 4, 2, 1):
        both = jnp.maximum(both, pltpu.roll(both, shift, 1))
    mine[...] = both
    theirs[0] = both

    def copy_to(step):
        return pltpu.make_async_remote_copy(
            src_ref=mine,
            dst_ref=theirs.at[step],
            send_sem=bsends.at[step],
            recv_sem=brecvs.at[step],
            device_id={"row": lax.rem(me + step, n)},
            device_id_type=pl.DeviceIdType.MESH,
        )

    for step in range(1, n):
        copy_to(step).start()

    def word_step(b, carry):
        rows = pad_rows(cols_ref[:, at_block(b)] >> 7)
        bits = [jnp.left_shift(1, row & 31) for row in rows]
        for q in range(4):
            word = jnp.where((rows[0] >> 5) == q, bits[0], 0) | jnp.where((rows[1] >> 5) == q, bits[1], 0)
            word = word[0:4] | word[4:8]
            word = word[0:2] | word[2:4]
            words[q, pl.ds(b, 1), :] = word[0:1] | word[1:2]
        return carry

    lax.fori_loop(0, blocks, word_step, 0, unroll=4)
    lane = lax.broadcasted_iota(i32, (blocks, LANE), 1)
    chosen = jnp.zeros((blocks, LANE), i32)
    for q in range(4):
        word = words[q]
        for shift in (64, 32, 16, 8, 4, 2, 1):
            word = word | pltpu.roll(word, shift, 1)
        chosen = jnp.where((lane >> 5) == q, word, chosen)
    present = (jnp.right_shift(chosen, lane & 31) & 1).astype(f32).astype(bf16)
    tri = (
        lax.broadcasted_iota(i32, (LANE, LANE), 0) <= lax.broadcasted_iota(i32, (LANE, LANE), 1)
    ).astype(f32).astype(bf16)
    upto = jnp.dot(present, tri, preferred_element_type=f32).astype(i32)
    for s in range(blocks // 8):
        count = upto[8 * s : 8 * s + 8]
        slot = lane[0:8]
        found = jnp.zeros((8, LANE), i32)
        for step in (64, 32, 16, 8, 4, 2, 1):
            there = take_lanes(count, found + (step - 1))
            found = jnp.where(there <= slot, found + step, found)
        total = take_lanes(count, jnp.full((8, LANE), LANE - 1, i32))
        lists_ref[8 * s : 8 * s + 8, :] = found + total * 256

    for step in range(1, n):
        copy_to(step).wait()
    bounds_ref[...] = jnp.max(theirs[...], axis=0)
    keep.wait()
    wait()


def apply_into(out_ref, lists_ref, table_ref, vals_ref, cols_ref):
    blocks = cols_ref.shape[1] // LANE

    def group_step(g, carry):
        base = g * GROUP
        index = [halves(cols_ref[:, at_block(base + u)]) for u in range(GROUP)]
        most = lists_ref[base, 0]
        for u in range(1, GROUP):
            most = jnp.maximum(most, lists_ref[base + u, 0])
        chunks = ((most >> 8) + (CHUNK - 1)) // CHUNK

        def chunk_step(k, flat):
            flat = list(flat)
            for u in range(GROUP):
                acc = flat[6 * u : 6 * u + 6]
                for t in range(CHUNK):
                    r = lists_ref[base + u, k * CHUNK + t] & 255
                    acc = visit(table_ref, r, *index[u], acc)
                flat[6 * u : 6 * u + 6] = acc
            return tuple(flat)

        zero = jnp.zeros((8, LANE), f32)
        flat = chunk_step(0, (zero,) * (6 * GROUP))
        flat = lax.fori_loop(1, chunks, chunk_step, flat)
        for u in range(GROUP):
            at = at_block(base + u)
            for c, row in enumerate(contract(vals_ref, at, flat[6 * u : 6 * u + 6])):
                out_ref[c : c + 1, at] = row
        return carry

    lax.fori_loop(0, blocks // GROUP, group_step, 0)


def apply_start(lists_ref, ext_ref, vals_ref, cols_ref, rhs_ref, dinv_ref, bounds_ref,
                res_ref, first_ref, scratch):
    apply_into(scratch, lists_ref, ext_ref, vals_ref, cols_ref)
    theta = coefficients(bounds_ref[0:1, 0:1])[0]
    res = rhs_ref[...] - scratch[...]
    res_ref[...] = res
    first_ref[...] = dinv_ref[...] * res / theta


def apply_first(lists_ref, ext_ref, vals_ref, cols_ref, res_ref, dinv_ref, bounds_ref, first_ref,
                start_ref, res_out, second_ref, iterate_ref, scratch):
    apply_into(scratch, lists_ref, ext_ref, vals_ref, cols_ref)
    theta, delta, rho_zero, rho_one = coefficients(bounds_ref[0:1, 0:1])
    res = res_ref[...] - scratch[...]
    res_out[...] = res
    first = first_ref[...]
    second = (rho_one * rho_zero) * first + (2.0 * rho_one / delta) * dinv_ref[...] * res
    second_ref[...] = second
    iterate_ref[...] = start_ref[...] + first + second


def apply_second(lists_ref, ext_ref, vals_ref, cols_ref, res_ref, prol_ref, place_ref,
                 sums_ref, scratch):
    apply_into(scratch, lists_ref, ext_ref, vals_ref, cols_ref)
    count = scratch.shape[1]
    tiles = sums_ref.shape[1] // LANE
    piece = 8 * LANE

    def step(p, acc):
        at = pl.ds(pl.multiple_of(p * piece, piece), piece)
        res = res_ref[:, at] - scratch[:, at]
        contrib = jnp.zeros((3, piece), f32)
        for c in range(3):
            contrib = contrib + prol_ref[c, :, at].astype(f32) * res[c : c + 1]
        head = contrib.astype(bf16).astype(f32)
        tail = contrib - head
        both = jnp.concatenate([head, tail, jnp.zeros((2, piece), f32)], axis=0)
        place = place_ref[:, at]
        high = jnp.broadcast_to(place >> 7, (8, piece))
        rows = jnp.concatenate([jnp.where(high == h, both, 0.0) for h in range(tiles)], axis=0)
        hot = jnp.where(
            jnp.broadcast_to(place & (LANE - 1), (LANE, piece))
            == lax.broadcasted_iota(i32, (LANE, piece), 0),
            1.0,
            0.0,
        ).astype(bf16)
        return acc + lax.dot_general(
            rows.astype(bf16), hot, (((1,), (1,)), ((), ())), preferred_element_type=f32
        )

    acc = lax.fori_loop(0, count // piece, step, jnp.zeros((8 * tiles, LANE), f32))
    for h in range(tiles):
        part = acc[8 * h : 8 * h + 8]
        sums_ref[:, h * LANE : (h + 1) * LANE] = part[0:3] + part[3:6]


def coarse_kernel(n, sums_ref, vals_ref, cols_ref, dinv_ref, bounds_ref,
                  iterate_ref, res_ref, ghosts, d1, d2, t1, t2, sends, recvs):
    me = lax.axis_index("row")
    own = dinv_ref.shape[1]
    blocks = own // LANE
    width = own // 2
    greet(me, n, False)
    wide = own + 2 * LANE
    low = pltpu.make_async_remote_copy(
        src_ref=sums_ref.at[:, pl.ds(0, LANE)], dst_ref=ghosts.at[1],
        send_sem=sends.at[0], recv_sem=recvs.at[0],
        device_id={"row": jnp.maximum(me - 1, 0)}, device_id_type=pl.DeviceIdType.MESH,
    )
    high = pltpu.make_async_remote_copy(
        src_ref=sums_ref.at[:, pl.ds(wide - LANE, LANE)], dst_ref=ghosts.at[0],
        send_sem=sends.at[1], recv_sem=recvs.at[1],
        device_id={"row": jnp.minimum(me + 1, n - 1)}, device_id_type=pl.DeviceIdType.MESH,
    )
    zeros = jnp.zeros((3, LANE), f32)

    @pl.when(me > 0)
    def _():
        low.start()

    @pl.when(me < n - 1)
    def _():
        high.start()

    @pl.when(me == 0)
    def _():
        ghosts[0] = zeros

    @pl.when(me == n - 1)
    def _():
        ghosts[1] = zeros

    index = [halves(cols_ref[:, at_block(b)]) for b in range(blocks)]
    theta, delta, rho_zero, rho_one = coefficients(bounds_ref[4:5, 0:1])
    dinv = dinv_ref[...]

    @pl.when(me > 0)
    def _():
        low.wait_send()
        high.wait_recv()

    @pl.when(me < n - 1)
    def _():
        high.wait_send()
        low.wait_recv()

    tiles = [sums_ref[:, (h + 1) * LANE : (h + 2) * LANE] for h in range(blocks)]
    tiles[0] = tiles[0] + ghosts[0]
    tiles[-1] = tiles[-1] + ghosts[1]
    res = jnp.concatenate(tiles, axis=1)

    def apply(table):
        for b in range(blocks):
            acc = [jnp.zeros((8, LANE), f32)] * 6
            for r in range(2 * blocks):
                acc = visit(table, r, *index[b], acc)
            for c, row in enumerate(contract(vals_ref, at_block(b), acc)):
                res_ref[c : c + 1, at_block(b)] = row

    def swap(value, held, table, k):
        held[...] = value
        start, wait = exchange(
            held, table, width, own, me, n, sends.at[pl.ds(2 * k, 2)], recvs.at[pl.ds(2 * k, 2)]
        )
        start()
        table[:, pl.ds(width, own)] = value
        wait()

    first = dinv * res / theta
    swap(first, d1, t1, 1)
    apply(t1)
    res = res - res_ref[...]
    second = (rho_one * rho_zero) * first + (2.0 * rho_one / delta) * dinv * res
    swap(second, d2, t2, 2)
    iterate_ref[...] = first + second
    apply(t2)
    res_ref[...] = res - res_ref[...]


def params(collective=None):
    if collective is None:
        return pltpu.CompilerParams(vmem_limit_bytes=48 * 1024 * 1024)
    return pltpu.CompilerParams(
        vmem_limit_bytes=48 * 1024 * 1024, collective_id=collective, has_side_effects=True
    )


def halo_kernel(n, vector_ref, ext_ref, sends, recvs, own_sem):
    me = lax.axis_index("row")
    own = vector_ref.shape[1]
    width = (ext_ref.shape[1] - own) // 2
    greet(me, n, False)
    start, wait = exchange(vector_ref, ext_ref, width, own, me, n, sends, recvs)
    start()
    keep = pltpu.make_async_copy(vector_ref, ext_ref.at[:, pl.ds(width, own)], own_sem)
    keep.start()
    keep.wait()
    wait()


def shards(n, start, rhs, fine_vals, fine_cols, prol, aggregate, coarse_vals, coarse_cols):
    nf, nc = start.shape[1], coarse_vals.shape[3]
    blocks = nf // LANE
    shape = jax.ShapeDtypeStruct
    fine, ext = shape((3, nf), f32), shape((3, 2 * nf), f32)
    coarse = shape((3, nc), f32)
    dma = pltpu.SemaphoreType.DMA

    ext0, lists, dinv, cdinv, bounds = pl.pallas_call(
        functools.partial(first_kernel, n),
        out_shape=(ext, shape((blocks, LANE), i32), fine, coarse, shape((8, LANE), f32)),
        in_specs=[VMEM] * 4,
        out_specs=(VMEM,) * 5,
        scratch_shapes=[
            pltpu.VMEM((4, blocks, LANE), i32),
            pltpu.VMEM((8, LANE), f32),
            pltpu.VMEM((n, 8, LANE), f32),
            dma((2,)), dma((2,)), dma((n,)), dma((n,)), dma,
        ],
        compiler_params=params(0),
        name="prepare",
    )(start, fine_vals, fine_cols, coarse_vals)

    def halo(vector, collective):
        return pl.pallas_call(
            functools.partial(halo_kernel, n),
            out_shape=ext,
            in_specs=[VMEM],
            out_specs=VMEM,
            scratch_shapes=[dma((2,)), dma((2,)), dma],
            compiler_params=params(collective),
            name=f"halo{collective}",
        )(vector)

    def applied(kernel, outs, *args):
        return pl.pallas_call(
            kernel,
            out_shape=outs,
            in_specs=[SMEM] + [VMEM] * len(args),
            out_specs=(VMEM,) * len(outs),
            scratch_shapes=[pltpu.VMEM((3, nf), f32)],
            compiler_params=params(),
            name=kernel.__name__,
        )(lists, *args)

    res, first = applied(
        apply_start, (fine, fine), ext0, fine_vals, fine_cols, rhs, dinv, bounds
    )
    res, second, iterate = applied(
        apply_first, (fine, fine, fine), halo(first, 1), fine_vals, fine_cols, res, dinv, bounds,
        first, start,
    )
    place = (aggregate - (lax.axis_index("row") * nc - LANE)).reshape(1, nf)
    (sums,) = applied(
        apply_second, (shape((3, nc + 2 * LANE), f32),), halo(second, 2), fine_vals, fine_cols, res,
        prol, place,
    )
    coarse_iterate, coarse_residual = pl.pallas_call(
        functools.partial(coarse_kernel, n),
        out_shape=(coarse, coarse),
        in_specs=[VMEM] * 5,
        out_specs=(VMEM,) * 2,
        scratch_shapes=[
            pltpu.VMEM((2, 3, LANE), f32),
            pltpu.VMEM((3, nc), f32), pltpu.VMEM((3, nc), f32),
            pltpu.VMEM((3, 2 * nc), f32), pltpu.VMEM((3, 2 * nc), f32),
            dma((6,)), dma((6,)),
        ],
        compiler_params=params(3),
        name="coarse",
    )(sums, coarse_vals, coarse_cols, cdinv, bounds)
    return (iterate, coarse_iterate, coarse_residual)


def solution(mesh):
    in_specs = (
        P(None, ("grp", "row")),
        P(None, ("grp", "row")),
        P(None, None, None, ("grp", "row")),
        P(None, ("grp", "row")),
        P(None, None, ("grp", "row")),
        P(("grp", "row")),
        P(None, None, None, ("grp", "row")),
        P(None, ("grp", "row")),
    )
    out_specs = (P(None, ("grp", "row")), P(None, ("grp", "row")), P(None, ("grp", "row")))
    return jax.shard_map(
        functools.partial(shards, mesh.shape["row"]),
        mesh=mesh, in_specs=in_specs, out_specs=out_specs, check_vma=False,
    )
```

time: 1270 us -> 84.8 us (0.07)
  local copies, waits for them, and re-layouts: 1130 us -> 7.31 us
  Pallas kernels: 0 us -> 75.6 us
  other arithmetic: 58.7 us -> 0.77 us
  starting transfers between devices: 43.6 us -> 0 us
  blocking collectives: 23.8 us -> 0 us
    gather x10 -> x0, local copies, waits for them, and re-layouts: 1110 us -> none  [local_apply(): gathered = extended[:, columns]]
    pallas_call x0 -> x7, Pallas kernels: none -> 75.6 us  [the longest x3 46.3 us: applied(): pl.pallas_call(kernel, out_shape=outs, in_specs=[SMEM] + [VMEM] * len(arg...]
    scatter-add x1 -> x0, other arithmetic: 44.5 us -> none  [shards(): jnp.zeros((3, 3 * NC), jnp.float32).at[:, position].add(contrib)]
    ppermute x12 -> x0, starting transfers between devices: 43.6 us -> none  [the longest x5 19.3 us: padded(): lax.ppermute(lax.slice_in_dim(block, 0, width, axis=dim), axis, backward)]
    pmax x1 -> x0, blocking collectives: 23.8 us -> none  [shards(): bound = lax.pmax(fine_local, 'row')]
    concatenate x5 -> x0, local copies, waits for them, and re-layouts: 17.1 us -> none  [padded(): block = jnp.concatenate([low, block, high], axis=dim)]
  transfers between devices with their start and end apart: 12 -> 0, of which waited for: 4 -> 0; matrix products, arithmetic and copies ran while one was open for 0% -> 0% of each run, Pallas kernels for 0% -> 0%
where the time goes in v1:
time: 84.8 us; the launch traced here: 84.5 us
  Pallas kernels  75.6 us (89%)
  local copies, waits for them, and re-layouts  7.31 us (9%)
    pallas_call x3, Pallas kernels, applied(): pl.pallas_call(kernel, out_shape=outs, in_specs=[SMEM] + [VMEM] * len(arg...  46.3 us
    pallas_call x1, Pallas kernels, shards(): pl.pallas_call(functools.partial(coarse_kernel, n), out_shape=(coarse, co...  10.2 us
    pallas_call x1, Pallas kernels, shards(): pl.pallas_call(functools.partial(first_kernel, n), out_shape=(ext, shape(...  9.79 us
    pallas_call x2, Pallas kernels, halo(): pl.pallas_call(functools.partial(halo_kernel, n), out_shape=ext, in_specs...  9.32 us
    unnamed x28, local copies, waits for them, and re-layouts  7.31 us

profile of v1, /device:TPU:7, one launch (start us, length us, event | category | flops | bytes accessed | tf_op | source)
XLA Modules:
  0.0 84.5 jit_solution(9770863576580681129)
XLA Ops:
  0.6 0.0 copy-start
  0.6 1.7 %copy-done = bf16[3,3,12,8192]{3,2,1,0:T(8,128)(2,1)S(1)} copy-done((bf16[3,3,12,8192]{3,2,1,0:T(8,128)(2,1)S(1)}, bf16[3,3,12,8192]{3,2,1,0:T(8,128)(2,1)}, u32[]{:S(2)}) %copy-start) | copy-done | bytes 1769496
  2.3 0.0 copy-start.2
  2.3 1.0 %copy-done.2 = s32[12,8192]{1,0:T(8,128)S(1)} copy-done((s32[12,8192]{1,0:T(8,128)S(1)}, s32[12,8192]{1,0:T(8,128)}, u32[]{:S(2)}) %copy-start.2) | copy-done | bytes 393240
  3.3 0.0 copy-start.4
  3.3 0.9 %copy-done.4 = bf16[3,3,12,512]{3,2,1,0:T(8,128)(2,1)S(1)} copy-done((bf16[3,3,12,512]{3,2,1,0:T(8,128)(2,1)S(1)}, bf16[3,3,12,512]{3,2,1,0:T(8,128)(2,1)}, u32[]{:S(2)}) %copy-start.4) | copy-done | bytes 110616
  4.2 0.0 copy-start.6
  4.3 0.9 %copy-done.6 = f32[3,8192]{1,0:T(4,128)S(1)} copy-done((f32[3,8192]{1,0:T(4,128)S(1)}, f32[3,8192]{1,0:T(4,128)}, u32[]{:S(2)}) %copy-start.6) | copy-done | bytes 98328
  5.2 0.0 copy-start.1
  5.2 0.0 copy-start.3
  5.2 9.8 %prepare.1 = (f32[3,16384]{1,0:T(4,128)S(1)}, s32[64,128]{1,0:T(8,128)S(1)}, f32[3,8192]{1,0:T(4,128)S(1)}, f32[3,512]{1,0:T(4,128)S(1)}, f32[8,128]{1,0:T(8,128)S(1)}) custom-call(f32[3,8192]{1,0:T(4,128)S(1)} %copy-done.6, bf16[3,3,12,8192]{3,2,1,0:T(8,128)(2,1)S(1)} %copy-done, s32[12,8192]{1,0:T(8,128)S(1)} %copy-done.2, ...), custom_call_target="tpu_custom_call" | custom-call | tf_op jit(solution)/shard_map/prepare/pallas_call | solution.py:445
  15.0 0.0 copy-start.7
  15.0 0.0 copy-done.1
  15.0 0.0 copy-done.3
  15.0 0.0 copy-done.11
  15.0 14.6 %apply_start.1 = (f32[3,8192]{1,0:T(4,128)S(1)}, f32[3,8192]{1,0:T(4,128)S(1)}) custom-call(s32[64,128]{1,0:T(8,128)S(1)} %get-tuple-element.15.lists_ref, f32[3,16384]{1,0:T(4,128)S(1)} %get-tuple-element.16.ext_ref, bf16[3,3,12,8192]{3,2,1,0:T(8,128)(2,1)S(1)} %copy-done.1, s32[12,8192]{1,0:T(8,128)S(1)} %copy-done.3, f32[3,8192]{1,0:T(4,128)S(1)} %copy-done.11, ...), custom_call_target="tpu_custom_call" | custom-call | tf_op jit(solution)/shard_map/apply_start/pallas_call | solution.py:472
  29.6 0.0 copy-start.8
  29.6 4.7 %halo1.1.ext_ref = f32[3,16384]{1,0:T(4,128)S(1)} custom-call(f32[3,8192]{1,0:T(4,128)S(1)} %get-tuple-element.19.vector_ref.first_ref), custom_call_target="tpu_custom_call" | custom-call | tf_op jit(solution)/shard_map/halo1/pallas_call | solution.py:461
  34.3 0.0 copy-done.7
  34.3 15.3 %apply_first.1 = (f32[3,8192]{1,0:T(4,128)S(1)}, f32[3,8192]{1,0:T(4,128)S(1)}, f32[3,8192]{1,0:T(4,128)}) custom-call(s32[64,128]{1,0:T(8,128)S(1)} %get-tuple-element.15.lists_ref, f32[3,16384]{1,0:T(4,128)S(1)} %halo1.1.ext_ref, bf16[3,3,12,8192]{3,2,1,0:T(8,128)(2,1)S(1)} %copy-done.1, s32[12,8192]{1,0:T(8,128)S(1)} %copy-done.3, ...), custom_call_target="tpu_custom_call" | custom-call | tf_op jit(solution)/shard_map/apply_first/pallas_call | solution.py:472
  49.6 0.7 copy-done.9
  50.2 4.6 %halo2.1.ext_ref = f32[3,16384]{1,0:T(4,128)S(1)} custom-call(f32[3,8192]{1,0:T(4,128)S(1)} %get-tuple-element.22.vector_ref), custom_call_target="tpu_custom_call" | custom-call | tf_op jit(solution)/shard_map/halo2/pallas_call | solution.py:461
  54.9 0.0 copy-start.12
  54.9 0.8 broadcast_subtract_fusion
  55.7 0.0 copy-done.8
  55.7 0.9 %copy-done.10 = f32[3,8192]{1,0:T(4,128)S(1)} copy-done((f32[3,8192]{1,0:T(4,128)S(1)}, f32[3,8192]{1,0:T(4,128)}, u32[]{:S(2)}) %copy-start.10) | copy-done | bytes 98328
  56.6 16.5 %apply_second.1.sums_ref = f32[3,768]{1,0:T(4,128)S(1)} custom-call(s32[64,128]{1,0:T(8,128)S(1)} %get-tuple-element.15.lists_ref, f32[3,16384]{1,0:T(4,128)S(1)} %halo2.1.ext_ref, bf16[3,3,12,8192]{3,2,1,0:T(8,128)(2,1)S(1)} %copy-done.1, s32[12,8192]{1,0:T(8,128)S(1)} %copy-done.3, f32[3,8192]{1,0:T(4,128)S(1)} %copy-done.10, ...), custom_call_target="tpu_custom_call" | custom-call | tf_op jit(solution)/shard_map/apply_second/pallas_call | solution.py:472
  73.1 0.0 copy-done.5
  73.1 0.0 copy-done.12
  73.1 10.2 %coarse.1 = (f32[3,512]{1,0:T(4,128)S(1)}, f32[3,512]{1,0:T(4,128)S(1)}) custom-call(f32[3,768]{1,0:T(4,128)S(1)} %apply_second.1.sums_ref, bf16[3,3,12,512]{3,2,1,0:T(8,128)(2,1)S(1)} %copy-done.5, s32[12,512]{1,0:T(8,128)S(1)} %copy-done.12, f32[3,512]{1,0:T(4,128)S(1)} %get-tuple-element.24.dinv_ref, f32[8,128]{1,0:T(8,128)S(1)} %get-tuple-element.18.bounds_ref), custom_call_target="tpu_custom_call" | custom-call | tf_op jit(solution)/shard_map/coarse/pallas_call | solution.py:494
  83.3 0.6 copy.13
  83.9 0.6 copy.14
  (4 shorter events, 0.0 us)
Async XLA Ops:
  0.6 1.7 %copy-start = (bf16[3,3,12,8192]{3,2,1,0:T(8,128)(2,1)S(1)}, bf16[3,3,12,8192]{3,2,1,0:T(8,128)(2,1)}, u32[]{:S(2)}) copy-start(bf16[3,3,12,8192]{3,2,1,0:T(8,128)(2,1)} %vals_ref.8) | copy-start | bytes 5308420
  2.3 1.0 %copy-start.2 = (s32[12,8192]{1,0:T(8,128)S(1)}, s32[12,8192]{1,0:T(8,128)}, u32[]{:S(2)}) copy-start(s32[12,8192]{1,0:T(8,128)} %cols_ref.8) | copy-start | bytes 1179652
  3.3 0.9 %copy-start.4 = (bf16[3,3,12,512]{3,2,1,0:T(8,128)(2,1)S(1)}, bf16[3,3,12,512]{3,2,1,0:T(8,128)(2,1)}, u32[]{:S(2)}) copy-start(bf16[3,3,12,512]{3,2,1,0:T(8,128)(2,1)} %vals_ref.9) | copy-start | bytes 331780
  4.2 0.9 %copy-start.6 = (f32[3,8192]{1,0:T(4,128)S(1)}, f32[3,8192]{1,0:T(4,128)}, u32[]{:S(2)}) copy-start(f32[3,8192]{1,0:T(4,128)} %start_ref.3) | copy-start | bytes 294916
  5.2 9.8 %copy-start.1 = (bf16[3,3,12,8192]{3,2,1,0:T(8,128)(2,1)S(1)}, bf16[3,3,12,8192]{3,2,1,0:T(8,128)(2,1)}, u32[]{:S(2)}) copy-start(bf16[3,3,12,8192]{3,2,1,0:T(8,128)(2,1)} %vals_ref.8) | copy-start | bytes 5308420
  5.2 9.8 %copy-start.3 = (s32[12,8192]{1,0:T(8,128)S(1)}, s32[12,8192]{1,0:T(8,128)}, u32[]{:S(2)}) copy-start(s32[12,8192]{1,0:T(8,128)} %cols_ref.8) | copy-start | bytes 1179652
  5.2 9.8 %copy-start.11 = (f32[3,8192]{1,0:T(4,128)S(1)}, f32[3,8192]{1,0:T(4,128)}, u32[]{:S(2)}) copy-start(f32[3,8192]{1,0:T(4,128)} %rhs_ref.1) | copy-start | bytes 294916
  15.0 19.3 %copy-start.7 = (f32[3,8192]{1,0:T(4,128)S(1)}, f32[3,8192]{1,0:T(4,128)}, u32[]{:S(2)}) copy-start(f32[3,8192]{1,0:T(4,128)} %start_ref.3) | copy-start | bytes 294916
  29.6 26.1 %copy-start.8 = (bf16[3,3,8192]{2,1,0:T(4,128)(2,1)S(1)}, bf16[3,3,8192]{2,1,0:T(4,128)(2,1)}, u32[]{:S(2)}) copy-start(bf16[3,3,8192]{2,1,0:T(4,128)(2,1)} %prol_ref.1) | copy-start | bytes 442372
  49.6 0.7 copy-start.9
  50.2 22.8 %copy-start.5 = (bf16[3,3,12,512]{3,2,1,0:T(8,128)(2,1)S(1)}, bf16[3,3,12,512]{3,2,1,0:T(8,128)(2,1)}, u32[]{:S(2)}) copy-start(bf16[3,3,12,512]{3,2,1,0:T(8,128)(2,1)} %vals_ref.9) | copy-start | bytes 331780
  54.9 18.2 %copy-start.12 = (s32[12,512]{1,0:T(8,128)S(1)}, s32[12,512]{1,0:T(8,128)}, u32[]{:S(2)}) copy-start(s32[12,512]{1,0:T(8,128)} %cols_ref.9) | copy-start | bytes 73732
  55.7 0.9 %copy-start.10 = (f32[3,8192]{1,0:T(4,128)S(1)}, f32[3,8192]{1,0:T(4,128)}, u32[]{:S(2)}) copy-start(f32[3,8192]{1,0:T(4,128)} %copy-done.9) | copy-start | bytes 294916

commit v2 on v1

--- a/solution.py
+++ b/solution.py
@@ -9,12 +9,14 @@
 
 LANE = 128
 CHUNK = 16
-GROUP = 4
+PAIRS = 2
+STEPS = float(2**20 - 1)
 lower_fraction = 0.1
 
 f32, i32, bf16 = jnp.float32, jnp.int32, jnp.bfloat16
 VMEM = pl.BlockSpec(memory_space=pltpu.VMEM)
 SMEM = pl.BlockSpec(memory_space=pltpu.SMEM)
+HBM = pl.BlockSpec(memory_space=pltpu.HBM)
 
 
 def coefficients(bound):
@@ -44,6 +46,47 @@
 def halves(cols):
     parts = pad_rows(cols)
     return [p & (LANE - 1) for p in parts], [p >> 7 for p in parts]
+
+
+def pair_index(cols_ref, p):
+    cols = [cols_ref[:, at_block(2 * p + u)] for u in range(2)]
+    rel = [((c >> 7) - (2 * p + u)) & (LANE - 1) for u, c in enumerate(cols)]
+    lanes = [c & (LANE - 1) for c in cols]
+    return [
+        (x[0][0:8], x[1][0:8], jnp.concatenate([x[0][8:12], x[1][8:12]], axis=0))
+        for x in (lanes, rel)
+    ]
+
+
+def visit_pair(table_ref, p, r, lanes, rows, upper, acc):
+    masks = [row == r for row in rows]
+    out = []
+    for w in range(2):
+        first, second = [
+            jnp.broadcast_to(table_ref[w : w + 1, at_block((2 * p + u + r) & (LANE - 1))], (8, LANE))
+            for u in range(2)
+        ]
+        for h, src in enumerate((first, second, jnp.where(upper, first, second))):
+            out.append(jnp.where(masks[h], take_lanes(src, lanes[h]), acc[3 * w + h]))
+    return out
+
+
+def pack(ext_ref, table_ref):
+    vector = ext_ref[...]
+    most = jnp.max(jnp.max(jnp.abs(vector), axis=1, keepdims=True), axis=0, keepdims=True)
+    most = jnp.maximum(most, 1e-30)
+    fixed = jnp.round(vector * (STEPS / most)).astype(i32)
+    third = fixed[2:3] + 2**20
+    table_ref[...] = jnp.left_shift(fixed[0:2], 11) | jnp.concatenate(
+        [third >> 10, third & 1023], axis=0
+    )
+    return most / STEPS
+
+
+def unpack(words):
+    one, two = words
+    third = (jnp.left_shift(one & 2047, 10) | (two & 1023)) - 2**20
+    return [x.astype(f32) for x in (one >> 11, two >> 11, third)]
 
 
 def visit(table_ref, r, lanes, rows, acc):
@@ -57,9 +100,8 @@
     return out
 
 
-def contract(vals_ref, at, acc):
+def contract(vals_ref, at, gathered):
     out = []
-    gathered = [jnp.concatenate([acc[2 * j], acc[2 * j + 1][0:4]], axis=0) for j in range(3)]
     for c in range(3):
         total = None
         for j in range(3):
@@ -136,7 +178,7 @@
     return start, wait
 
 
-def greet(me, n, everyone):
+def greet(me, n, everyone, between=lambda: None):
     barrier = pltpu.get_barrier_semaphore()
     if everyone:
         def one(step, carry):
@@ -147,6 +189,7 @@
             return carry
 
         lax.fori_loop(1, n, one, 0)
+        between()
         pl.semaphore_wait(barrier, n - 1)
     else:
         for cond, who in neighbours(me, n):
@@ -155,38 +198,58 @@
                 pl.semaphore_signal(
                     barrier, inc=1, device_id={"row": who}, device_id_type=pl.DeviceIdType.MESH
                 )
+        between()
         pl.semaphore_wait(barrier, jnp.minimum(me, 1) + jnp.minimum(n - 1 - me, 1))
 
 
-def first_kernel(n, start_ref, vals_ref, cols_ref, cvals_ref,
+def first_kernel(n, start_hbm, vals_hbm, cols_hbm, cvals_hbm,
                  ext_ref, lists_ref, dinv_ref, cdinv_ref, bounds_ref,
-                 words, mine, theirs, sends, recvs, bsends, brecvs, own_sem):
+                 vals_ref, cols_ref, cvals_ref, words, mine, theirs,
+                 sends, recvs, bsends, brecvs, local):
     me = lax.axis_index("row")
-    own = start_ref.shape[1]
+    own = start_hbm.shape[1]
     width = (ext_ref.shape[1] - own) // 2
     blocks, cblocks = own // LANE, cvals_ref.shape[3] // LANE
-    greet(me, n, True)
-    start, wait = exchange(start_ref, ext_ref, width, own, me, n, sends, recvs)
+    part = own // 4
+    fetch_vals = [
+        pltpu.make_async_copy(
+            vals_hbm.at[:, :, :, pl.ds(p * part, part)],
+            vals_ref.at[:, :, :, pl.ds(p * part, part)],
+            local.at[p],
+        )
+        for p in range(4)
+    ]
+    fetch_cvals = pltpu.make_async_copy(cvals_hbm, cvals_ref, local.at[4])
+    fetch_cols = pltpu.make_async_copy(cols_hbm, cols_ref, local.at[5])
+    keep = pltpu.make_async_copy(start_hbm, ext_ref.at[:, pl.ds(width, own)], local.at[6])
+    for copy in (*fetch_vals, fetch_cvals, fetch_cols, keep):
+        copy.start()
+    start, wait = exchange(start_hbm, ext_ref, width, own, me, n, sends, recvs)
+
+    def bounds():
+        low = jnp.full((1, LANE), -jnp.inf, f32)
+
+        def bound_step(g, best):
+            for u in range(4):
+                best = bound_of_block(vals_ref, at_block(g * 4 + u), dinv_ref, best)
+            return best
+
+        best = low
+        for p in range(4):
+            fetch_vals[p].wait()
+            best = lax.fori_loop(p * (blocks // 16), (p + 1) * (blocks // 16), bound_step, best)
+        fetch_cvals.wait()
+        cbest = low
+        for b in range(cblocks):
+            cbest = bound_of_block(cvals_ref, at_block(b), cdinv_ref, cbest)
+        both = jnp.concatenate([jnp.broadcast_to(x, (4, LANE)) for x in (best, cbest)], axis=0)
+        for shift in (64, 32, 16, 8, 4, 2, 1):
+            both = jnp.maximum(both, pltpu.roll(both, shift, 1))
+        mine[...] = both
+        theirs[0] = both
+
+    greet(me, n, True, bounds)
     start()
-    keep = pltpu.make_async_copy(start_ref, ext_ref.at[:, pl.ds(width, own)], own_sem)
-    keep.start()
-
-    low = jnp.full((1, LANE), -jnp.inf, f32)
-
-    def bound_step(g, best):
-        for u in range(2):
-            best = bound_of_block(vals_ref, at_block(g * 2 + u), dinv_ref, best)
-        return best
-
-    best = lax.fori_loop(0, blocks // 2, bound_step, low)
-    cbest = low
-    for b in range(cblocks):
-        cbest = bound_of_block(cvals_ref, at_block(b), cdinv_ref, cbest)
-    both = jnp.concatenate([jnp.broadcast_to(x, (4, LANE)) for x in (best, cbest)], axis=0)
-    for shift in (64, 32, 16, 8, 4, 2, 1):
-        both = jnp.maximum(both, pltpu.roll(both, shift, 1))
-    mine[...] = both
-    theirs[0] = both
 
     def copy_to(step):
         return pltpu.make_async_remote_copy(
@@ -201,19 +264,24 @@
     for step in range(1, n):
         copy_to(step).start()
 
-    def word_step(b, carry):
-        rows = pad_rows(cols_ref[:, at_block(b)] >> 7)
+    fetch_cols.wait()
+    pairs = blocks // 2
+
+    def word_step(p, carry):
+        _, rows = pair_index(cols_ref, p)
         bits = [jnp.left_shift(1, row & 31) for row in rows]
         for q in range(4):
-            word = jnp.where((rows[0] >> 5) == q, bits[0], 0) | jnp.where((rows[1] >> 5) == q, bits[1], 0)
+            word = functools.reduce(
+                jnp.bitwise_or, [jnp.where((rows[h] >> 5) == q, bits[h], 0) for h in range(3)]
+            )
             word = word[0:4] | word[4:8]
             word = word[0:2] | word[2:4]
-            words[q, pl.ds(b, 1), :] = word[0:1] | word[1:2]
+            words[q, pl.ds(p, 1), :] = word[0:1] | word[1:2]
         return carry
 
-    lax.fori_loop(0, blocks, word_step, 0, unroll=4)
-    lane = lax.broadcasted_iota(i32, (blocks, LANE), 1)
-    chosen = jnp.zeros((blocks, LANE), i32)
+    lax.fori_loop(0, pairs, word_step, 0, unroll=4)
+    lane = lax.broadcasted_iota(i32, (pairs, LANE), 1)
+    chosen = jnp.zeros((pairs, LANE), i32)
     for q in range(4):
         word = words[q]
         for shift in (64, 32, 16, 8, 4, 2, 1):
@@ -224,7 +292,7 @@
         lax.broadcasted_iota(i32, (LANE, LANE), 0) <= lax.broadcasted_iota(i32, (LANE, LANE), 1)
     ).astype(f32).astype(bf16)
     upto = jnp.dot(present, tri, preferred_element_type=f32).astype(i32)
-    for s in range(blocks // 8):
+    for s in range(pairs // 8):
         count = upto[8 * s : 8 * s + 8]
         slot = lane[0:8]
         found = jnp.zeros((8, LANE), i32)
@@ -241,53 +309,61 @@
     wait()
 
 
-def apply_into(out_ref, lists_ref, table_ref, vals_ref, cols_ref):
-    blocks = cols_ref.shape[1] // LANE
+def apply_into(out_ref, table_ref, lists_ref, ext_ref, vals_ref, cols_ref):
+    unit = pack(ext_ref, table_ref)
+    upper = lax.broadcasted_iota(i32, (8, LANE), 0) < 4
 
     def group_step(g, carry):
-        base = g * GROUP
-        index = [halves(cols_ref[:, at_block(base + u)]) for u in range(GROUP)]
+        base = g * PAIRS
+        index = [pair_index(cols_ref, base + u) for u in range(PAIRS)]
         most = lists_ref[base, 0]
-        for u in range(1, GROUP):
+        for u in range(1, PAIRS):
             most = jnp.maximum(most, lists_ref[base + u, 0])
         chunks = ((most >> 8) + (CHUNK - 1)) // CHUNK
 
         def chunk_step(k, flat):
             flat = list(flat)
-            for u in range(GROUP):
+            for u in range(PAIRS):
                 acc = flat[6 * u : 6 * u + 6]
                 for t in range(CHUNK):
                     r = lists_ref[base + u, k * CHUNK + t] & 255
-                    acc = visit(table_ref, r, *index[u], acc)
+                    acc = visit_pair(table_ref, base + u, r, *index[u], upper, acc)
                 flat[6 * u : 6 * u + 6] = acc
             return tuple(flat)
 
-        zero = jnp.zeros((8, LANE), f32)
-        flat = chunk_step(0, (zero,) * (6 * GROUP))
+        zero = jnp.zeros((8, LANE), i32)
+        flat = chunk_step(0, (zero,) * (6 * PAIRS))
         flat = lax.fori_loop(1, chunks, chunk_step, flat)
-        for u in range(GROUP):
-            at = at_block(base + u)
-            for c, row in enumerate(contract(vals_ref, at, flat[6 * u : 6 * u + 6])):
-                out_ref[c : c + 1, at] = row
+        for u in range(PAIRS):
+            parts = [unpack((flat[6 * u + h], flat[6 * u + 3 + h])) for h in range(3)]
+            for v in range(2):
+                at = at_block(2 * (base + u) + v)
+                gathered = [
+                    jnp.concatenate([parts[v][j], parts[2][j][4 * v : 4 * v + 4]], axis=0)
+                    for j in range(3)
+                ]
+                for c, row in enumerate(contract(vals_ref, at, gathered)):
+                    out_ref[c : c + 1, at] = row
         return carry
 
-    lax.fori_loop(0, blocks // GROUP, group_step, 0)
+    lax.fori_loop(0, cols_ref.shape[1] // (2 * LANE * PAIRS), group_step, 0)
+    return unit
 
 
 def apply_start(lists_ref, ext_ref, vals_ref, cols_ref, rhs_ref, dinv_ref, bounds_ref,
-                res_ref, first_ref, scratch):
-    apply_into(scratch, lists_ref, ext_ref, vals_ref, cols_ref)
+                res_ref, first_ref, scratch, table):
+    unit = apply_into(scratch, table, lists_ref, ext_ref, vals_ref, cols_ref)
     theta = coefficients(bounds_ref[0:1, 0:1])[0]
-    res = rhs_ref[...] - scratch[...]
+    res = rhs_ref[...] - unit * scratch[...]
     res_ref[...] = res
     first_ref[...] = dinv_ref[...] * res / theta
 
 
 def apply_first(lists_ref, ext_ref, vals_ref, cols_ref, res_ref, dinv_ref, bounds_ref, first_ref,
-                start_ref, res_out, second_ref, iterate_ref, scratch):
-    apply_into(scratch, lists_ref, ext_ref, vals_ref, cols_ref)
+                start_ref, res_out, second_ref, iterate_ref, scratch, table):
+    unit = apply_into(scratch, table, lists_ref, ext_ref, vals_ref, cols_ref)
     theta, delta, rho_zero, rho_one = coefficients(bounds_ref[0:1, 0:1])
-    res = res_ref[...] - scratch[...]
+    res = res_ref[...] - unit * scratch[...]
     res_out[...] = res
     first = first_ref[...]
     second = (rho_one * rho_zero) * first + (2.0 * rho_one / delta) * dinv_ref[...] * res
@@ -296,22 +372,23 @@
 
 
 def apply_second(lists_ref, ext_ref, vals_ref, cols_ref, res_ref, prol_ref, place_ref,
-                 sums_ref, scratch):
-    apply_into(scratch, lists_ref, ext_ref, vals_ref, cols_ref)
+                 sums_ref, scratch, table):
+    unit = apply_into(scratch, table, lists_ref, ext_ref, vals_ref, cols_ref)
     count = scratch.shape[1]
     tiles = sums_ref.shape[1] // LANE
     piece = 8 * LANE
+    offset = lax.axis_index("row") * (sums_ref.shape[1] - 2 * LANE) - LANE
 
     def step(p, acc):
         at = pl.ds(pl.multiple_of(p * piece, piece), piece)
-        res = res_ref[:, at] - scratch[:, at]
+        res = res_ref[:, at] - unit * scratch[:, at]
         contrib = jnp.zeros((3, piece), f32)
         for c in range(3):
             contrib = contrib + prol_ref[c, :, at].astype(f32) * res[c : c + 1]
         head = contrib.astype(bf16).astype(f32)
         tail = contrib - head
         both = jnp.concatenate([head, tail, jnp.zeros((2, piece), f32)], axis=0)
-        place = place_ref[:, at]
+        place = place_ref[:, at] - offset
         high = jnp.broadcast_to(place >> 7, (8, piece))
         rows = jnp.concatenate([jnp.where(high == h, both, 0.0) for h in range(tiles)], axis=0)
         hot = jnp.where(
@@ -390,7 +467,8 @@
             acc = [jnp.zeros((8, LANE), f32)] * 6
             for r in range(2 * blocks):
                 acc = visit(table, r, *index[b], acc)
-            for c, row in enumerate(contract(vals_ref, at_block(b), acc)):
+            gathered = [jnp.concatenate([acc[2 * j], acc[2 * j + 1][0:4]], axis=0) for j in range(3)]
+            for c, row in enumerate(contract(vals_ref, at_block(b), gathered)):
                 res_ref[c : c + 1, at_block(b)] = row
 
     def swap(value, held, table, k):
@@ -415,9 +493,9 @@
 
 def params(collective=None):
     if collective is None:
-        return pltpu.CompilerParams(vmem_limit_bytes=48 * 1024 * 1024)
+        return pltpu.CompilerParams(vmem_limit_bytes=24 * 1024 * 1024)
     return pltpu.CompilerParams(
-        vmem_limit_bytes=48 * 1024 * 1024, collective_id=collective, has_side_effects=True
+        vmem_limit_bytes=24 * 1024 * 1024, collective_id=collective, has_side_effects=True
     )
 
 
@@ -444,14 +522,17 @@
 
     ext0, lists, dinv, cdinv, bounds = pl.pallas_call(
         functools.partial(first_kernel, n),
-        out_shape=(ext, shape((blocks, LANE), i32), fine, coarse, shape((8, LANE), f32)),
-        in_specs=[VMEM] * 4,
+        out_shape=(ext, shape((blocks // 2, LANE), i32), fine, coarse, shape((8, LANE), f32)),
+        in_specs=[HBM] * 4,
         out_specs=(VMEM,) * 5,
         scratch_shapes=[
-            pltpu.VMEM((4, blocks, LANE), i32),
+            pltpu.VMEM(fine_vals.shape, bf16),
+            pltpu.VMEM(fine_cols.shape, i32),
+            pltpu.VMEM(coarse_vals.shape, bf16),
+            pltpu.VMEM((4, blocks // 2, LANE), i32),
             pltpu.VMEM((8, LANE), f32),
             pltpu.VMEM((n, 8, LANE), f32),
-            dma((2,)), dma((2,)), dma((n,)), dma((n,)), dma,
+            dma((2,)), dma((2,)), dma((n,)), dma((n,)), dma((7,)),
         ],
         compiler_params=params(0),
         name="prepare",
@@ -474,7 +555,7 @@
             out_shape=outs,
             in_specs=[SMEM] + [VMEM] * len(args),
             out_specs=(VMEM,) * len(outs),
-            scratch_shapes=[pltpu.VMEM((3, nf), f32)],
+            scratch_shapes=[pltpu.VMEM((3, nf), f32), pltpu.VMEM((2, 2 * nf), i32)],
             compiler_params=params(),
             name=kernel.__name__,
         )(lists, *args)
@@ -486,7 +567,7 @@
         apply_first, (fine, fine, fine), halo(first, 1), fine_vals, fine_cols, res, dinv, bounds,
         first, start,
     )
-    place = (aggregate - (lax.axis_index("row") * nc - LANE)).reshape(1, nf)
+    place = aggregate.reshape(1, nf)
     (sums,) = applied(
         apply_second, (shape((3, nc + 2 * LANE), f32),), halo(second, 2), fine_vals, fine_cols, res,
         prol, place,

time: 84.8 us -> 71.7 us (0.85)
  Pallas kernels: 75.6 us -> 64.9 us
  local copies, waits for them, and re-layouts: 7.31 us -> 5.75 us
    pallas_call x3, Pallas kernels: 46.3 us -> 36 us  [applied(): pl.pallas_call(kernel, out_shape=outs, in_specs=[SMEM] + [VMEM] * len(arg...]
    unnamed x28 -> x26, local copies, waits for them, and re-layouts: 7.31 us -> 5.75 us
where the time goes in v2:
time: 71.7 us; the launch traced here: 71.4 us
  Pallas kernels  64.9 us (91%)
  local copies, waits for them, and re-layouts  5.75 us (8%)
  between operations  0.78 us (1%)
    pallas_call x3, Pallas kernels, applied(): pl.pallas_call(kernel, out_shape=outs, in_specs=[SMEM] + [VMEM] * len(arg...  36 us
    pallas_call x1, Pallas kernels, shards(): pl.pallas_call(functools.partial(coarse_kernel, n), out_shape=(coarse, co...  10.2 us
    pallas_call x1, Pallas kernels, shards(): pl.pallas_call(functools.partial(first_kernel, n), out_shape=(ext, shape(...  9.38 us
    pallas_call x2, Pallas kernels, halo(): pl.pallas_call(functools.partial(halo_kernel, n), out_shape=ext, in_specs...  9.32 us
    unnamed x26, local copies, waits for them, and re-layouts  5.75 us

profile of v2, /device:TPU:7, one launch (start us, length us, event | category | flops | bytes accessed | tf_op | source)
XLA Modules:
  0.0 71.4 jit_solution(12913070771705320543)
XLA Ops:
  0.6 0.0 copy-start
  0.6 1.7 %copy-done = bf16[3,3,12,8192]{3,2,1,0:T(8,128)(2,1)S(1)} copy-done((bf16[3,3,12,8192]{3,2,1,0:T(8,128)(2,1)S(1)}, bf16[3,3,12,8192]{3,2,1,0:T(8,128)(2,1)}, u32[]{:S(2)}) %copy-start) | copy-done | bytes 1769496
  2.3 0.0 copy-start.2
  2.3 1.0 %copy-done.2 = s32[12,8192]{1,0:T(8,128)S(1)} copy-done((s32[12,8192]{1,0:T(8,128)S(1)}, s32[12,8192]{1,0:T(8,128)}, u32[]{:S(2)}) %copy-start.2) | copy-done | bytes 393240
  3.3 0.0 copy-start.4
  3.3 0.9 %copy-done.4 = bf16[3,3,12,512]{3,2,1,0:T(8,128)(2,1)S(1)} copy-done((bf16[3,3,12,512]{3,2,1,0:T(8,128)(2,1)S(1)}, bf16[3,3,12,512]{3,2,1,0:T(8,128)(2,1)}, u32[]{:S(2)}) %copy-start.4) | copy-done | bytes 110616
  4.2 0.0 copy-start.6
  4.3 0.9 %copy-done.6 = f32[3,8192]{1,0:T(4,128)S(1)} copy-done((f32[3,8192]{1,0:T(4,128)S(1)}, f32[3,8192]{1,0:T(4,128)}, u32[]{:S(2)}) %copy-start.6) | copy-done | bytes 98328
  5.2 0.0 copy-start.1
  5.2 0.0 copy-start.3
  5.2 0.0 copy-start.9
  5.2 9.4 %prepare.1 = (f32[3,16384]{1,0:T(4,128)S(1)}, s32[32,128]{1,0:T(8,128)S(1)}, f32[3,8192]{1,0:T(4,128)S(1)}, f32[3,512]{1,0:T(4,128)S(1)}, f32[8,128]{1,0:T(8,128)S(1)}) custom-call(f32[3,8192]{1,0:T(4,128)S(1)} %copy-done.6, bf16[3,3,12,8192]{3,2,1,0:T(8,128)(2,1)S(1)} %copy-done, s32[12,8192]{1,0:T(8,128)S(1)} %copy-done.2, ...), custom_call_target="tpu_custom_call" | custom-call | tf_op jit(solution)/shard_map/prepare/pallas_call | solution.py:523
  14.5 0.0 copy-start.7
  14.6 0.0 copy-done.1
  14.6 0.0 copy-done.3
  14.6 0.0 copy-done.9
  14.6 11.1 %apply_start.1 = (f32[3,8192]{1,0:T(4,128)S(1)}, f32[3,8192]{1,0:T(4,128)S(1)}) custom-call(s32[32,128]{1,0:T(8,128)S(1)} %get-tuple-element.15.lists_ref, f32[3,16384]{1,0:T(4,128)S(1)} %get-tuple-element.16.ext_ref, bf16[3,3,12,8192]{3,2,1,0:T(8,128)(2,1)S(1)} %copy-done.1, s32[12,8192]{1,0:T(8,128)S(1)} %copy-done.3, f32[3,8192]{1,0:T(4,128)S(1)} %copy-done.9, ...), custom_call_target="tpu_custom_call" | custom-call | tf_op jit(solution)/shard_map/apply_start/pallas_call | solution.py:553
  25.7 0.0 copy-start.8
  25.7 0.0 copy-start.10
  25.8 4.7 %halo1.1.ext_ref = f32[3,16384]{1,0:T(4,128)S(1)} custom-call(f32[3,8192]{1,0:T(4,128)S(1)} %get-tuple-element.19.vector_ref.first_ref), custom_call_target="tpu_custom_call" | custom-call | tf_op jit(solution)/shard_map/halo1/pallas_call | solution.py:542
  30.5 0.0 copy-done.7
  30.5 11.8 %apply_first.1 = (f32[3,8192]{1,0:T(4,128)S(1)}, f32[3,8192]{1,0:T(4,128)S(1)}, f32[3,8192]{1,0:T(4,128)}) custom-call(s32[32,128]{1,0:T(8,128)S(1)} %get-tuple-element.15.lists_ref, f32[3,16384]{1,0:T(4,128)S(1)} %halo1.1.ext_ref, bf16[3,3,12,8192]{3,2,1,0:T(8,128)(2,1)S(1)} %copy-done.1, s32[12,8192]{1,0:T(8,128)S(1)} %copy-done.3, ...), custom_call_target="tpu_custom_call" | custom-call | tf_op jit(solution)/shard_map/apply_first/pallas_call | solution.py:553
  42.3 0.0 copy-start.5
  42.3 4.6 %halo2.1.ext_ref = f32[3,16384]{1,0:T(4,128)S(1)} custom-call(f32[3,8192]{1,0:T(4,128)S(1)} %get-tuple-element.22.vector_ref), custom_call_target="tpu_custom_call" | custom-call | tf_op jit(solution)/shard_map/halo2/pallas_call | solution.py:542
  47.0 0.0 copy-done.8
  47.0 0.0 copy-done.10
  47.0 13.1 %apply_second.1.sums_ref = f32[3,768]{1,0:T(4,128)S(1)} custom-call(s32[32,128]{1,0:T(8,128)S(1)} %get-tuple-element.15.lists_ref, f32[3,16384]{1,0:T(4,128)S(1)} %halo2.1.ext_ref, bf16[3,3,12,8192]{3,2,1,0:T(8,128)(2,1)S(1)} %copy-done.1, s32[12,8192]{1,0:T(8,128)S(1)} %copy-done.3, f32[3,8192]{1,0:T(4,128)S(1)} %get-tuple-element.23.res_ref, ...), custom_call_target="tpu_custom_call" | custom-call | tf_op jit(solution)/shard_map/apply_second/pallas_call | solution.py:553
  60.0 0.0 copy-done.5
  60.0 0.0 copy-done.11
  60.1 10.2 %coarse.1 = (f32[3,512]{1,0:T(4,128)S(1)}, f32[3,512]{1,0:T(4,128)S(1)}) custom-call(f32[3,768]{1,0:T(4,128)S(1)} %apply_second.1.sums_ref, bf16[3,3,12,512]{3,2,1,0:T(8,128)(2,1)S(1)} %copy-done.5, s32[12,512]{1,0:T(8,128)S(1)} %copy-done.11, f32[3,512]{1,0:T(4,128)S(1)} %get-tuple-element.24.dinv_ref, f32[8,128]{1,0:T(8,128)S(1)} %get-tuple-element.18.bounds_ref), custom_call_target="tpu_custom_call" | custom-call | tf_op jit(solution)/shard_map/coarse/pallas_call | solution.py:575
  70.2 0.6 copy.13
  70.8 0.6 copy.14
  (1 shorter events, 0.0 us)
Async XLA Ops:
  0.6 1.7 %copy-start = (bf16[3,3,12,8192]{3,2,1,0:T(8,128)(2,1)S(1)}, bf16[3,3,12,8192]{3,2,1,0:T(8,128)(2,1)}, u32[]{:S(2)}) copy-start(bf16[3,3,12,8192]{3,2,1,0:T(8,128)(2,1)} %vals_ref.6) | copy-start | bytes 5308420
  2.3 1.0 %copy-start.2 = (s32[12,8192]{1,0:T(8,128)S(1)}, s32[12,8192]{1,0:T(8,128)}, u32[]{:S(2)}) copy-start(s32[12,8192]{1,0:T(8,128)} %cols_ref.6) | copy-start | bytes 1179652
  3.3 0.9 %copy-start.4 = (bf16[3,3,12,512]{3,2,1,0:T(8,128)(2,1)S(1)}, bf16[3,3,12,512]{3,2,1,0:T(8,128)(2,1)}, u32[]{:S(2)}) copy-start(bf16[3,3,12,512]{3,2,1,0:T(8,128)(2,1)} %vals_ref.7) | copy-start | bytes 331780
  4.2 0.9 %copy-start.6 = (f32[3,8192]{1,0:T(4,128)S(1)}, f32[3,8192]{1,0:T(4,128)}, u32[]{:S(2)}) copy-start(f32[3,8192]{1,0:T(4,128)} %start_ref.1) | copy-start | bytes 294916
  5.2 9.4 %copy-start.1 = (bf16[3,3,12,8192]{3,2,1,0:T(8,128)(2,1)S(1)}, bf16[3,3,12,8192]{3,2,1,0:T(8,128)(2,1)}, u32[]{:S(2)}) copy-start(bf16[3,3,12,8192]{3,2,1,0:T(8,128)(2,1)} %vals_ref.6) | copy-start | bytes 5308420
  5.2 9.4 %copy-start.3 = (s32[12,8192]{1,0:T(8,128)S(1)}, s32[12,8192]{1,0:T(8,128)}, u32[]{:S(2)}) copy-start(s32[12,8192]{1,0:T(8,128)} %cols_ref.6) | copy-start | bytes 1179652
  5.2 9.4 %copy-start.9 = (f32[3,8192]{1,0:T(4,128)S(1)}, f32[3,8192]{1,0:T(4,128)}, u32[]{:S(2)}) copy-start(f32[3,8192]{1,0:T(4,128)} %rhs_ref.1) | copy-start | bytes 294916
  14.5 15.9 %copy-start.7 = (f32[3,8192]{1,0:T(4,128)S(1)}, f32[3,8192]{1,0:T(4,128)}, u32[]{:S(2)}) copy-start(f32[3,8192]{1,0:T(4,128)} %start_ref.1) | copy-start | bytes 294916
  25.7 21.2 %copy-start.8 = (bf16[3,3,8192]{2,1,0:T(4,128)(2,1)S(1)}, bf16[3,3,8192]{2,1,0:T(4,128)(2,1)}, u32[]{:S(2)}) copy-start(bf16[3,3,8192]{2,1,0:T(4,128)(2,1)} %prol_ref.1) | copy-start | bytes 442372
  25.7 21.2 %copy-start.10 = (s32[8192]{0:T(1024)S(1)}, s32[8192]{0:T(1024)}, u32[]{:S(2)}) copy-start(s32[8192]{0:T(1024)} %param.13) | copy-start | bytes 98308
  42.3 17.7 %copy-start.5 = (bf16[3,3,12,512]{3,2,1,0:T(8,128)(2,1)S(1)}, bf16[3,3,12,512]{3,2,1,0:T(8,128)(2,1)}, u32[]{:S(2)}) copy-start(bf16[3,3,12,512]{3,2,1,0:T(8,128)(2,1)} %vals_ref.7) | copy-start | bytes 331780
  42.3 17.7 %copy-start.11 = (s32[12,512]{1,0:T(8,128)S(1)}, s32[12,512]{1,0:T(8,128)}, u32[]{:S(2)}) copy-start(s32[12,512]{1,0:T(8,128)} %cols_ref.7) | copy-start | bytes 73732

commit v3 on v2

--- a/solution.py
+++ b/solution.py
@@ -50,7 +50,7 @@
 
 def pair_index(cols_ref, p):
     cols = [cols_ref[:, at_block(2 * p + u)] for u in range(2)]
-    rel = [((c >> 7) - (2 * p + u)) & (LANE - 1) for u, c in enumerate(cols)]
+    rel = [((c >> 7) - u) & (LANE - 1) for u, c in enumerate(cols)]
     lanes = [c & (LANE - 1) for c in cols]
     return [
         (x[0][0:8], x[1][0:8], jnp.concatenate([x[0][8:12], x[1][8:12]], axis=0))
@@ -58,28 +58,49 @@
     ]
 
 
-def visit_pair(table_ref, p, r, lanes, rows, upper, acc):
-    masks = [row == r for row in rows]
-    out = []
-    for w in range(2):
-        first, second = [
-            jnp.broadcast_to(table_ref[w : w + 1, at_block((2 * p + u + r) & (LANE - 1))], (8, LANE))
-            for u in range(2)
-        ]
-        for h, src in enumerate((first, second, jnp.where(upper, first, second))):
-            out.append(jnp.where(masks[h], take_lanes(src, lanes[h]), acc[3 * w + h]))
-    return out
+def visit_pair(table_ref, wanted, lanes, rows, upper, acc):
+    acc = list(acc)
+    for h in range(3):
+        for r in wanted:
+            mask = rows[h] == r
+            for w in range(2):
+                two = table_ref[w : w + 1, pl.ds(pl.multiple_of(r * LANE, LANE), 2 * LANE)]
+                first = jnp.broadcast_to(two[:, :LANE], (8, LANE))
+                second = jnp.broadcast_to(two[:, LANE:], (8, LANE))
+                src = (first, second, None)[h]
+                if src is None:
+                    src = jnp.where(upper, first, second)
+                acc[3 * w + h] = jnp.where(mask, take_lanes(src, lanes[h]), acc[3 * w + h])
+    return acc
 
 
 def pack(ext_ref, table_ref):
-    vector = ext_ref[...]
-    most = jnp.max(jnp.max(jnp.abs(vector), axis=1, keepdims=True), axis=0, keepdims=True)
+    size = ext_ref.shape[1]
+    piece = 16 * LANE
+
+    def at(p):
+        return pl.ds(pl.multiple_of(p * piece, piece), piece)
+
+    def largest(p, most):
+        return jnp.maximum(most, jnp.abs(ext_ref[:, at(p)]))
+
+    most = lax.fori_loop(0, size // piece, largest, jnp.zeros((3, piece), f32))
+    most = jnp.max(jnp.max(most, axis=1, keepdims=True), axis=0, keepdims=True)
     most = jnp.maximum(most, 1e-30)
-    fixed = jnp.round(vector * (STEPS / most)).astype(i32)
-    third = fixed[2:3] + 2**20
-    table_ref[...] = jnp.left_shift(fixed[0:2], 11) | jnp.concatenate(
-        [third >> 10, third & 1023], axis=0
-    )
+    scale = STEPS / most
+
+    def words(vector):
+        fixed = jnp.round(vector * scale).astype(i32)
+        third = jnp.broadcast_to(fixed[2:3] + 2**20, (2, vector.shape[1]))
+        head = lax.broadcasted_iota(i32, third.shape, 0) == 0
+        return jnp.left_shift(fixed[0:2], 11) | jnp.where(head, third >> 10, third & 1023)
+
+    def step(p, carry):
+        table_ref[:, at(p)] = words(ext_ref[:, at(p)])
+        return carry
+
+    lax.fori_loop(0, size // piece, step, 0)
+    table_ref[:, size : size + LANE] = table_ref[:, 0:LANE]
     return most / STEPS
 
 
@@ -300,7 +321,8 @@
             there = take_lanes(count, found + (step - 1))
             found = jnp.where(there <= slot, found + step, found)
         total = take_lanes(count, jnp.full((8, LANE), LANE - 1, i32))
-        lists_ref[8 * s : 8 * s + 8, :] = found + total * 256
+        lists_ref[8 * s : 8 * s + 8, :] = found
+        lists_ref[pairs + 8 * s : pairs + 8 * s + 8, :] = total
 
     for step in range(1, n):
         copy_to(step).wait()
@@ -316,19 +338,19 @@
     def group_step(g, carry):
         base = g * PAIRS
         index = [pair_index(cols_ref, base + u) for u in range(PAIRS)]
-        most = lists_ref[base, 0]
+        pairs = cols_ref.shape[1] // (2 * LANE)
+        most = lists_ref[pairs + base, 0]
         for u in range(1, PAIRS):
-            most = jnp.maximum(most, lists_ref[base + u, 0])
-        chunks = ((most >> 8) + (CHUNK - 1)) // CHUNK
+            most = jnp.maximum(most, lists_ref[pairs + base + u, 0])
+        chunks = (most + (CHUNK - 1)) // CHUNK
 
         def chunk_step(k, flat):
             flat = list(flat)
             for u in range(PAIRS):
-                acc = flat[6 * u : 6 * u + 6]
-                for t in range(CHUNK):
-                    r = lists_ref[base + u, k * CHUNK + t] & 255
-                    acc = visit_pair(table_ref, base + u, r, *index[u], upper, acc)
-                flat[6 * u : 6 * u + 6] = acc
+                wanted = [lists_ref[base + u, k * CHUNK + t] for t in range(CHUNK)]
+                flat[6 * u : 6 * u + 6] = visit_pair(
+                    table_ref, wanted, *index[u], upper, flat[6 * u : 6 * u + 6]
+                )
             return tuple(flat)
 
         zero = jnp.zeros((8, LANE), i32)
@@ -407,8 +429,20 @@
         sums_ref[:, h * LANE : (h + 1) * LANE] = part[0:3] + part[3:6]
 
 
+def apply_coarse(table, vals_ref, cols_ref, out_ref):
+    blocks = cols_ref.shape[1] // LANE
+    for b in range(blocks):
+        lanes, rows = halves(cols_ref[:, at_block(b)])
+        acc = [jnp.zeros((8, LANE), f32)] * 6
+        for r in range(2 * blocks):
+            acc = visit(table, r, lanes, rows, acc)
+        gathered = [jnp.concatenate([acc[2 * j], acc[2 * j + 1][0:4]], axis=0) for j in range(3)]
+        for c, row in enumerate(contract(vals_ref, at_block(b), gathered)):
+            out_ref[c : c + 1, at_block(b)] = row
+
+
 def coarse_kernel(n, sums_ref, vals_ref, cols_ref, dinv_ref, bounds_ref,
-                  iterate_ref, res_ref, ghosts, d1, d2, t1, t2, sends, recvs):
+                  t2, first_ref, res_ref, ghosts, d1, d2, t1, sends, recvs):
     me = lax.axis_index("row")
     own = dinv_ref.shape[1]
     blocks = own // LANE
@@ -443,7 +477,6 @@
     def _():
         ghosts[1] = zeros
 
-    index = [halves(cols_ref[:, at_block(b)]) for b in range(blocks)]
     theta, delta, rho_zero, rho_one = coefficients(bounds_ref[4:5, 0:1])
     dinv = dinv_ref[...]
 
@@ -461,15 +494,6 @@
     tiles[0] = tiles[0] + ghosts[0]
     tiles[-1] = tiles[-1] + ghosts[1]
     res = jnp.concatenate(tiles, axis=1)
-
-    def apply(table):
-        for b in range(blocks):
-            acc = [jnp.zeros((8, LANE), f32)] * 6
-            for r in range(2 * blocks):
-                acc = visit(table, r, *index[b], acc)
-            gathered = [jnp.concatenate([acc[2 * j], acc[2 * j + 1][0:4]], axis=0) for j in range(3)]
-            for c, row in enumerate(contract(vals_ref, at_block(b), gathered)):
-                res_ref[c : c + 1, at_block(b)] = row
 
     def swap(value, held, table, k):
         held[...] = value
@@ -482,20 +506,26 @@
 
     first = dinv * res / theta
     swap(first, d1, t1, 1)
-    apply(t1)
+    first_ref[...] = first
+    apply_coarse(t1, vals_ref, cols_ref, res_ref)
     res = res - res_ref[...]
+    res_ref[...] = res
     second = (rho_one * rho_zero) * first + (2.0 * rho_one / delta) * dinv * res
     swap(second, d2, t2, 2)
-    iterate_ref[...] = first + second
-    apply(t2)
-    res_ref[...] = res - res_ref[...]
-
-
-def params(collective=None):
+
+
+def coarse_last(t2, vals_ref, cols_ref, first_ref, res_ref, iterate_ref, out_ref):
+    own = first_ref.shape[1]
+    iterate_ref[...] = first_ref[...] + t2[:, own // 2 : own // 2 + own]
+    apply_coarse(t2, vals_ref, cols_ref, out_ref)
+    out_ref[...] = res_ref[...] - out_ref[...]
+
+
+def params(collective=None, limit=24 * 1024 * 1024):
     if collective is None:
-        return pltpu.CompilerParams(vmem_limit_bytes=24 * 1024 * 1024)
+        return pltpu.CompilerParams(vmem_limit_bytes=limit)
     return pltpu.CompilerParams(
-        vmem_limit_bytes=24 * 1024 * 1024, collective_id=collective, has_side_effects=True
+        vmem_limit_bytes=limit, collective_id=collective, has_side_effects=True
     )
 
 
@@ -520,21 +550,22 @@
     coarse = shape((3, nc), f32)
     dma = pltpu.SemaphoreType.DMA
 
-    ext0, lists, dinv, cdinv, bounds = pl.pallas_call(
+    ext0, lists, dinv, cdinv, bounds, vals, cols, cvals = pl.pallas_call(
         functools.partial(first_kernel, n),
-        out_shape=(ext, shape((blocks // 2, LANE), i32), fine, coarse, shape((8, LANE), f32)),
+        out_shape=(
+            ext, shape((blocks, LANE), i32), fine, coarse, shape((8, LANE), f32),
+            shape(fine_vals.shape, bf16), shape(fine_cols.shape, i32),
+            shape(coarse_vals.shape, bf16),
+        ),
         in_specs=[HBM] * 4,
-        out_specs=(VMEM,) * 5,
+        out_specs=(VMEM,) * 8,
         scratch_shapes=[
-            pltpu.VMEM(fine_vals.shape, bf16),
-            pltpu.VMEM(fine_cols.shape, i32),
-            pltpu.VMEM(coarse_vals.shape, bf16),
             pltpu.VMEM((4, blocks // 2, LANE), i32),
             pltpu.VMEM((8, LANE), f32),
             pltpu.VMEM((n, 8, LANE), f32),
             dma((2,)), dma((2,)), dma((n,)), dma((n,)), dma((7,)),
         ],
-        compiler_params=params(0),
+        compiler_params=params(0, 52_000_000),
         name="prepare",
     )(start, fine_vals, fine_cols, coarse_vals)
 
@@ -555,37 +586,45 @@
             out_shape=outs,
             in_specs=[SMEM] + [VMEM] * len(args),
             out_specs=(VMEM,) * len(outs),
-            scratch_shapes=[pltpu.VMEM((3, nf), f32), pltpu.VMEM((2, 2 * nf), i32)],
+            scratch_shapes=[pltpu.VMEM((3, nf), f32), pltpu.VMEM((2, 2 * nf + LANE), i32)],
             compiler_params=params(),
             name=kernel.__name__,
         )(lists, *args)
 
     res, first = applied(
-        apply_start, (fine, fine), ext0, fine_vals, fine_cols, rhs, dinv, bounds
+        apply_start, (fine, fine), ext0, vals, cols, rhs, dinv, bounds
     )
     res, second, iterate = applied(
-        apply_first, (fine, fine, fine), halo(first, 1), fine_vals, fine_cols, res, dinv, bounds,
+        apply_first, (fine, fine, fine), halo(first, 1), vals, cols, res, dinv, bounds,
         first, start,
     )
     place = aggregate.reshape(1, nf)
     (sums,) = applied(
-        apply_second, (shape((3, nc + 2 * LANE), f32),), halo(second, 2), fine_vals, fine_cols, res,
+        apply_second, (shape((3, nc + 2 * LANE), f32),), halo(second, 2), vals, cols, res,
         prol, place,
     )
-    coarse_iterate, coarse_residual = pl.pallas_call(
+    table, first, res = pl.pallas_call(
         functools.partial(coarse_kernel, n),
-        out_shape=(coarse, coarse),
+        out_shape=(shape((3, 2 * nc), f32), coarse, coarse),
         in_specs=[VMEM] * 5,
-        out_specs=(VMEM,) * 2,
+        out_specs=(VMEM,) * 3,
         scratch_shapes=[
             pltpu.VMEM((2, 3, LANE), f32),
             pltpu.VMEM((3, nc), f32), pltpu.VMEM((3, nc), f32),
-            pltpu.VMEM((3, 2 * nc), f32), pltpu.VMEM((3, 2 * nc), f32),
+            pltpu.VMEM((3, 2 * nc), f32),
             dma((6,)), dma((6,)),
         ],
         compiler_params=params(3),
         name="coarse",
-    )(sums, coarse_vals, coarse_cols, cdinv, bounds)
+    )(sums, cvals, coarse_cols, cdinv, bounds)
+    coarse_iterate, coarse_residual = pl.pallas_call(
+        coarse_last,
+        out_shape=(coarse, coarse),
+        in_specs=[VMEM] * 5,
+        out_specs=(VMEM,) * 2,
+        compiler_params=params(),
+        name="coarse_last",
+    )(table, cvals, coarse_cols, first, res)
     return (iterate, coarse_iterate, coarse_residual)
 
 

time: 71.7 us -> 57.4 us (0.80)
  Pallas kernels: 64.9 us -> 53.6 us
  local copies, waits for them, and re-layouts: 5.75 us -> 2.87 us
    pallas_call x3, Pallas kernels: 36 us -> 24.2 us  [applied(): pl.pallas_call(kernel, out_shape=outs, in_specs=[SMEM] + [VMEM] * len(arg...]
    unnamed x26 -> x14, local copies, waits for them, and re-layouts: 5.75 us -> 2.87 us
    pallas_call x1 -> x2, Pallas kernels: 10.2 us -> 10.8 us  [the longest x1 9.75 us: shards(): pl.pallas_call(functools.partial(coarse_kernel, n), out_shape=(shape((3,...]
where the time goes in v3:
time: 57.4 us; the launch traced here: 57.2 us
  Pallas kernels  53.6 us (93%)
  local copies, waits for them, and re-layouts  2.87 us (5%)
  between operations  0.74 us (1%)
    pallas_call x3, Pallas kernels, applied(): pl.pallas_call(kernel, out_shape=outs, in_specs=[SMEM] + [VMEM] * len(arg...  24.2 us
    pallas_call x1, Pallas kernels, shards(): pl.pallas_call(functools.partial(coarse_kernel, n), out_shape=(shape((3,...  9.75 us
    pallas_call x2, Pallas kernels, halo(): pl.pallas_call(functools.partial(halo_kernel, n), out_shape=ext, in_specs...  9.32 us
    pallas_call x1, Pallas kernels, shards(): pl.pallas_call(functools.partial(first_kernel, n), out_shape=(ext, shape(...  9.22 us
    unnamed x14, local copies, waits for them, and re-layouts  2.87 us

profile of v3, /device:TPU:7, one launch (start us, length us, event | category | flops | bytes accessed | tf_op | source)
XLA Modules:
  0.0 57.2 jit_solution(14949143149689883772)
XLA Ops:
  0.6 0.0 copy-start
  0.6 0.9 %copy-done = f32[3,8192]{1,0:T(4,128)S(1)} copy-done((f32[3,8192]{1,0:T(4,128)S(1)}, f32[3,8192]{1,0:T(4,128)}, u32[]{:S(2)}) %copy-start) | copy-done | bytes 98328
  1.5 0.0 copy-start.1
  1.5 1.0 %copy-done.1 = s32[12,8192]{1,0:T(8,128)S(1)} copy-done((s32[12,8192]{1,0:T(8,128)S(1)}, s32[12,8192]{1,0:T(8,128)}, u32[]{:S(2)}) %copy-start.1) | copy-done | bytes 393240
  2.6 0.0 copy-start.3
  2.6 0.9 %copy-done.3 = bf16[3,3,12,512]{3,2,1,0:T(8,128)(2,1)S(1)} copy-done((bf16[3,3,12,512]{3,2,1,0:T(8,128)(2,1)S(1)}, bf16[3,3,12,512]{3,2,1,0:T(8,128)(2,1)}, u32[]{:S(2)}) %copy-start.3) | copy-done | bytes 110616
  3.5 0.0 copy-start.5
  3.5 9.2 %prepare.1 = (f32[3,16384]{1,0:T(4,128)S(1)}, s32[64,128]{1,0:T(8,128)S(1)}, f32[3,8192]{1,0:T(4,128)S(1)}, f32[3,512]{1,0:T(4,128)S(1)}, f32[8,128]{1,0:T(8,128...) custom-call(f32[3,8192]{1,0:T(4,128)S(1)} %copy-done, ...), custom_call_target="tpu_custom_call" | custom-call | tf_op jit(solution)/shard_map/prepare/pallas_call | solution.py:553
  12.7 0.0 copy-done.5
  12.7 7.2 %apply_start.1 = (f32[3,8192]{1,0:T(4,128)S(1)}, f32[3,8192]{1,0:T(4,128)S(1)}) custom-call(s32[64,128]{1,0:T(8,128)S(1)} %get-tuple-element.21.lists_ref, f32[3,16384]{1,0:T(4,128)S(1)} %get-tuple-element.22.ext_ref, bf16[3,3,12,8192]{3,2,1,0:T(8,128)(2,1)S(1)} %get-tuple-element.23.vals_ref, s32[12,8192]{1,0:T(8,128)S(1)} %get-tuple-element.24.cols_ref, ...), custom_call_target="tpu_custom_call" | custom-call | tf_op jit(solution)/shard_map/apply_start/pallas_call | solution.py:584
  19.9 0.0 copy-start.2
  20.0 0.0 copy-start.6
  20.0 4.7 %halo1.1.ext_ref = f32[3,16384]{1,0:T(4,128)S(1)} custom-call(f32[3,8192]{1,0:T(4,128)S(1)} %get-tuple-element.27.vector_ref.first_ref), custom_call_target="tpu_custom_call" | custom-call | tf_op jit(solution)/shard_map/halo1/pallas_call | solution.py:573
  24.7 7.9 %apply_first.1 = (f32[3,8192]{1,0:T(4,128)S(1)}, f32[3,8192]{1,0:T(4,128)S(1)}, f32[3,8192]{1,0:T(4,128)}) custom-call(s32[64,128]{1,0:T(8,128)S(1)} %get-tuple-element.21.lists_ref, f32[3,16384]{1,0:T(4,128)S(1)} %halo1.1.ext_ref, bf16[3,3,12,8192]{3,2,1,0:T(8,128)(2,1)S(1)} %get-tuple-element.23.vals_ref, s32[12,8192]{1,0:T(8,128)S(1)} %get-tuple-element.24.cols_ref, ...), custom_call_target="tpu_custom_call" | custom-call | tf_op jit(solution)/shard_map/apply_first/pallas_call | solution.py:584
  32.6 0.0 copy-start.4
  32.6 4.6 %halo2.1.ext_ref = f32[3,16384]{1,0:T(4,128)S(1)} custom-call(f32[3,8192]{1,0:T(4,128)S(1)} %get-tuple-element.30.vector_ref), custom_call_target="tpu_custom_call" | custom-call | tf_op jit(solution)/shard_map/halo2/pallas_call | solution.py:573
  37.2 0.0 copy-done.2
  37.2 0.0 copy-done.6
  37.2 9.1 %apply_second.1.sums_ref = f32[3,768]{1,0:T(4,128)S(1)} custom-call(s32[64,128]{1,0:T(8,128)S(1)} %get-tuple-element.21.lists_ref, f32[3,16384]{1,0:T(4,128)S(1)} %halo2.1.ext_ref, bf16[3,3,12,8192]{3,2,1,0:T(8,128)(2,1)S(1)} %get-tuple-element.23.vals_ref, s32[12,8192]{1,0:T(8,128)S(1)} %get-tuple-element.24.cols_ref, ...), custom_call_target="tpu_custom_call" | custom-call | tf_op jit(solution)/shard_map/apply_second/pallas_call | solution.py:584
  46.4 0.0 copy-done.4
  46.4 9.7 %coarse.1 = (f32[3,1024]{1,0:T(4,128)S(1)}, f32[3,512]{1,0:T(4,128)S(1)}, f32[3,512]{1,0:T(4,128)S(1)}) custom-call(f32[3,768]{1,0:T(4,128)S(1)} %apply_second.1.sums_ref, bf16[3,3,12,512]{3,2,1,0:T(8,128)(2,1)S(1)} %get-tuple-element.32.vals_ref, s32[12,512]{1,0:T(8,128)S(1)} %copy-done.4, f32[3,512]{1,0:T(4,128)S(1)} %get-tuple-element.33.dinv_ref, ...), custom_call_target="tpu_custom_call" | custom-call | tf_op jit(solution)/shard_map/coarse/pallas_call | solution.py:606
  56.1 1.0 %coarse_last.1 = (f32[3,512]{1,0:T(4,128)}, f32[3,512]{1,0:T(4,128)}) custom-call(f32[3,1024]{1,0:T(4,128)S(1)} %get-tuple-element.34.t2, bf16[3,3,12,512]{3,2,1,0:T(8,128)(2,1)S(1)} %get-tuple-element.32.vals_ref, s32[12,512]{1,0:T(8,128)S(1)} %copy-done.4, f32[3,512]{1,0:T(4,128)S(1)} %get-tuple-element.35.first_ref, f32[3,512]{1,0:T(4,128)S(1)} %get-tuple-element.36.res_ref), custom_call_target="tpu_custom_call" | custom-call | tf_op jit(solution)/shard_map/coarse_last/pallas_call | solution.py:620
Async XLA Ops:
  0.6 0.9 %copy-start = (f32[3,8192]{1,0:T(4,128)S(1)}, f32[3,8192]{1,0:T(4,128)}, u32[]{:S(2)}) copy-start(f32[3,8192]{1,0:T(4,128)} %start_ref.1) | copy-start | bytes 294916
  1.5 1.0 %copy-start.1 = (s32[12,8192]{1,0:T(8,128)S(1)}, s32[12,8192]{1,0:T(8,128)}, u32[]{:S(2)}) copy-start(s32[12,8192]{1,0:T(8,128)} %cols_hbm.1) | copy-start | bytes 1179652
  2.6 0.9 %copy-start.3 = (bf16[3,3,12,512]{3,2,1,0:T(8,128)(2,1)S(1)}, bf16[3,3,12,512]{3,2,1,0:T(8,128)(2,1)}, u32[]{:S(2)}) copy-start(bf16[3,3,12,512]{3,2,1,0:T(8,128)(2,1)} %cvals_hbm.1) | copy-start | bytes 331780
  3.5 9.2 %copy-start.5 = (f32[3,8192]{1,0:T(4,128)S(1)}, f32[3,8192]{1,0:T(4,128)}, u32[]{:S(2)}) copy-start(f32[3,8192]{1,0:T(4,128)} %rhs_ref.1) | copy-start | bytes 294916
  19.9 17.3 %copy-start.2 = (bf16[3,3,8192]{2,1,0:T(4,128)(2,1)S(1)}, bf16[3,3,8192]{2,1,0:T(4,128)(2,1)}, u32[]{:S(2)}) copy-start(bf16[3,3,8192]{2,1,0:T(4,128)(2,1)} %prol_ref.1) | copy-start | bytes 442372
  20.0 17.3 %copy-start.6 = (s32[8192]{0:T(1024)S(1)}, s32[8192]{0:T(1024)}, u32[]{:S(2)}) copy-start(s32[8192]{0:T(1024)} %param.13) | copy-start | bytes 98308
  32.6 13.8 %copy-start.4 = (s32[12,512]{1,0:T(8,128)S(1)}, s32[12,512]{1,0:T(8,128)}, u32[]{:S(2)}) copy-start(s32[12,512]{1,0:T(8,128)} %cols_ref.3) | copy-start | bytes 73732

commit v4 on v3

--- a/solution.py
+++ b/solution.py
@@ -8,8 +8,8 @@
 from jax.sharding import PartitionSpec as P
 
 LANE = 128
-CHUNK = 16
-PAIRS = 2
+CHUNK = 15
+PAIRS = 4
 STEPS = float(2**20 - 1)
 lower_fraction = 0.1
 
@@ -347,7 +347,10 @@
         def chunk_step(k, flat):
             flat = list(flat)
             for u in range(PAIRS):
-                wanted = [lists_ref[base + u, k * CHUNK + t] for t in range(CHUNK)]
+                wanted = [
+                    lists_ref[base + u, t if isinstance(k, int) else jnp.minimum(k * CHUNK + t, LANE - 1)]
+                    for t in range(CHUNK)
+                ]
                 flat[6 * u : 6 * u + 6] = visit_pair(
                     table_ref, wanted, *index[u], upper, flat[6 * u : 6 * u + 6]
                 )

time: 57.4 us -> 54.9 us (0.956)
  Pallas kernels: 53.6 us -> 51 us
    pallas_call x3, Pallas kernels: 24.2 us -> 21.7 us  [applied(): pl.pallas_call(kernel, out_shape=outs, in_specs=[SMEM] + [VMEM] * len(arg...]
where the time goes in v4:
time: 54.9 us; the launch traced here: 54.7 us
  Pallas kernels  51 us (93%)
  local copies, waits for them, and re-layouts  2.87 us (5%)
  between operations  0.74 us (1%)
    pallas_call x3, Pallas kernels, applied(): pl.pallas_call(kernel, out_shape=outs, in_specs=[SMEM] + [VMEM] * len(arg...  21.7 us
    pallas_call x1, Pallas kernels, shards(): pl.pallas_call(functools.partial(coarse_kernel, n), out_shape=(shape((3,...  9.75 us
    pallas_call x2, Pallas kernels, halo(): pl.pallas_call(functools.partial(halo_kernel, n), out_shape=ext, in_specs...  9.32 us
    pallas_call x1, Pallas kernels, shards(): pl.pallas_call(functools.partial(first_kernel, n), out_shape=(ext, shape(...  9.22 us
    unnamed x14, local copies, waits for them, and re-layouts  2.87 us

profile of v4, /device:TPU:7, one launch (start us, length us, event | category | flops | bytes accessed | tf_op | source)
XLA Modules:
  0.0 54.7 jit_solution(6899757110361074965)
XLA Ops:
  0.6 0.0 copy-start
  0.6 0.9 %copy-done = f32[3,8192]{1,0:T(4,128)S(1)} copy-done((f32[3,8192]{1,0:T(4,128)S(1)}, f32[3,8192]{1,0:T(4,128)}, u32[]{:S(2)}) %copy-start) | copy-done | bytes 98328
  1.5 0.0 copy-start.1
  1.5 1.0 %copy-done.1 = s32[12,8192]{1,0:T(8,128)S(1)} copy-done((s32[12,8192]{1,0:T(8,128)S(1)}, s32[12,8192]{1,0:T(8,128)}, u32[]{:S(2)}) %copy-start.1) | copy-done | bytes 393240
  2.6 0.0 copy-start.3
  2.6 0.9 %copy-done.3 = bf16[3,3,12,512]{3,2,1,0:T(8,128)(2,1)S(1)} copy-done((bf16[3,3,12,512]{3,2,1,0:T(8,128)(2,1)S(1)}, bf16[3,3,12,512]{3,2,1,0:T(8,128)(2,1)}, u32[]{:S(2)}) %copy-start.3) | copy-done | bytes 110616
  3.5 0.0 copy-start.5
  3.5 9.2 %prepare.1 = (f32[3,16384]{1,0:T(4,128)S(1)}, s32[64,128]{1,0:T(8,128)S(1)}, f32[3,8192]{1,0:T(4,128)S(1)}, f32[3,512]{1,0:T(4,128)S(1)}, f32[8,128]{1,0:T(8,128...) custom-call(f32[3,8192]{1,0:T(4,128)S(1)} %copy-done, ...), custom_call_target="tpu_custom_call" | custom-call | tf_op jit(solution)/shard_map/prepare/pallas_call | solution.py:556
  12.7 0.0 copy-done.5
  12.7 6.4 %apply_start.1 = (f32[3,8192]{1,0:T(4,128)S(1)}, f32[3,8192]{1,0:T(4,128)S(1)}) custom-call(s32[64,128]{1,0:T(8,128)S(1)} %get-tuple-element.21.lists_ref, f32[3,16384]{1,0:T(4,128)S(1)} %get-tuple-element.22.ext_ref, bf16[3,3,12,8192]{3,2,1,0:T(8,128)(2,1)S(1)} %get-tuple-element.23.vals_ref, s32[12,8192]{1,0:T(8,128)S(1)} %get-tuple-element.24.cols_ref, ...), custom_call_target="tpu_custom_call" | custom-call | tf_op jit(solution)/shard_map/apply_start/pallas_call | solution.py:587
  19.1 0.0 copy-start.2
  19.1 0.0 copy-start.6
  19.1 4.7 %halo1.1.ext_ref = f32[3,16384]{1,0:T(4,128)S(1)} custom-call(f32[3,8192]{1,0:T(4,128)S(1)} %get-tuple-element.27.vector_ref.first_ref), custom_call_target="tpu_custom_call" | custom-call | tf_op jit(solution)/shard_map/halo1/pallas_call | solution.py:576
  23.8 7.1 %apply_first.1 = (f32[3,8192]{1,0:T(4,128)S(1)}, f32[3,8192]{1,0:T(4,128)S(1)}, f32[3,8192]{1,0:T(4,128)}) custom-call(s32[64,128]{1,0:T(8,128)S(1)} %get-tuple-element.21.lists_ref, f32[3,16384]{1,0:T(4,128)S(1)} %halo1.1.ext_ref, bf16[3,3,12,8192]{3,2,1,0:T(8,128)(2,1)S(1)} %get-tuple-element.23.vals_ref, s32[12,8192]{1,0:T(8,128)S(1)} %get-tuple-element.24.cols_ref, ...), custom_call_target="tpu_custom_call" | custom-call | tf_op jit(solution)/shard_map/apply_first/pallas_call | solution.py:587
  30.9 0.0 copy-start.4
  30.9 4.6 %halo2.1.ext_ref = f32[3,16384]{1,0:T(4,128)S(1)} custom-call(f32[3,8192]{1,0:T(4,128)S(1)} %get-tuple-element.30.vector_ref), custom_call_target="tpu_custom_call" | custom-call | tf_op jit(solution)/shard_map/halo2/pallas_call | solution.py:576
  35.5 0.0 copy-done.2
  35.5 0.0 copy-done.6
  35.6 8.3 %apply_second.1.sums_ref = f32[3,768]{1,0:T(4,128)S(1)} custom-call(s32[64,128]{1,0:T(8,128)S(1)} %get-tuple-element.21.lists_ref, f32[3,16384]{1,0:T(4,128)S(1)} %halo2.1.ext_ref, bf16[3,3,12,8192]{3,2,1,0:T(8,128)(2,1)S(1)} %get-tuple-element.23.vals_ref, s32[12,8192]{1,0:T(8,128)S(1)} %get-tuple-element.24.cols_ref, ...), custom_call_target="tpu_custom_call" | custom-call | tf_op jit(solution)/shard_map/apply_second/pallas_call | solution.py:587
  43.8 0.0 copy-done.4
  43.9 9.7 %coarse.1 = (f32[3,1024]{1,0:T(4,128)S(1)}, f32[3,512]{1,0:T(4,128)S(1)}, f32[3,512]{1,0:T(4,128)S(1)}) custom-call(f32[3,768]{1,0:T(4,128)S(1)} %apply_second.1.sums_ref, bf16[3,3,12,512]{3,2,1,0:T(8,128)(2,1)S(1)} %get-tuple-element.32.vals_ref, s32[12,512]{1,0:T(8,128)S(1)} %copy-done.4, f32[3,512]{1,0:T(4,128)S(1)} %get-tuple-element.33.dinv_ref, ...), custom_call_target="tpu_custom_call" | custom-call | tf_op jit(solution)/shard_map/coarse/pallas_call | solution.py:609
  53.6 1.0 %coarse_last.1 = (f32[3,512]{1,0:T(4,128)}, f32[3,512]{1,0:T(4,128)}) custom-call(f32[3,1024]{1,0:T(4,128)S(1)} %get-tuple-element.34.t2, bf16[3,3,12,512]{3,2,1,0:T(8,128)(2,1)S(1)} %get-tuple-element.32.vals_ref, s32[12,512]{1,0:T(8,128)S(1)} %copy-done.4, f32[3,512]{1,0:T(4,128)S(1)} %get-tuple-element.35.first_ref, f32[3,512]{1,0:T(4,128)S(1)} %get-tuple-element.36.res_ref), custom_call_target="tpu_custom_call" | custom-call | tf_op jit(solution)/shard_map/coarse_last/pallas_call | solution.py:623
Async XLA Ops:
  0.6 0.9 %copy-start = (f32[3,8192]{1,0:T(4,128)S(1)}, f32[3,8192]{1,0:T(4,128)}, u32[]{:S(2)}) copy-start(f32[3,8192]{1,0:T(4,128)} %start_ref.1) | copy-start | bytes 294916
  1.5 1.0 %copy-start.1 = (s32[12,8192]{1,0:T(8,128)S(1)}, s32[12,8192]{1,0:T(8,128)}, u32[]{:S(2)}) copy-start(s32[12,8192]{1,0:T(8,128)} %cols_hbm.1) | copy-start | bytes 1179652
  2.6 0.9 %copy-start.3 = (bf16[3,3,12,512]{3,2,1,0:T(8,128)(2,1)S(1)}, bf16[3,3,12,512]{3,2,1,0:T(8,128)(2,1)}, u32[]{:S(2)}) copy-start(bf16[3,3,12,512]{3,2,1,0:T(8,128)(2,1)} %cvals_hbm.1) | copy-start | bytes 331780
  3.5 9.2 %copy-start.5 = (f32[3,8192]{1,0:T(4,128)S(1)}, f32[3,8192]{1,0:T(4,128)}, u32[]{:S(2)}) copy-start(f32[3,8192]{1,0:T(4,128)} %rhs_ref.1) | copy-start | bytes 294916
  19.1 16.4 %copy-start.2 = (bf16[3,3,8192]{2,1,0:T(4,128)(2,1)S(1)}, bf16[3,3,8192]{2,1,0:T(4,128)(2,1)}, u32[]{:S(2)}) copy-start(bf16[3,3,8192]{2,1,0:T(4,128)(2,1)} %prol_ref.1) | copy-start | bytes 442372
  19.1 16.4 %copy-start.6 = (s32[8192]{0:T(1024)S(1)}, s32[8192]{0:T(1024)}, u32[]{:S(2)}) copy-start(s32[8192]{0:T(1024)} %param.13) | copy-start | bytes 98308
  30.9 12.9 %copy-start.4 = (s32[12,512]{1,0:T(8,128)S(1)}, s32[12,512]{1,0:T(8,128)}, u32[]{:S(2)}) copy-start(s32[12,512]{1,0:T(8,128)} %cols_ref.3) | copy-start | bytes 73732
